TPU v7x, 32 devices: a whole 2x2x4 slice. The times are simulated.
32 devices in a mesh: fsdp: 16 (over z, y, core), tp: 2 (over x).
Axes of the slice: x: 2, y: 2, z: 4, core: 2. Of those that a mesh axis runs over, the one named last changes fastest.
Arguments:
- tokens: bfloat16 [16, 512, 768], P('fsdp', 'tp'), may hold values from -6 to 6
- segments: int32 [16, 512], P('fsdp'), may hold values from 0 to 2, as said below
- valid: int32 [16, 512], P('fsdp', 'tp'), may hold values from 0 to 1, as said below
- teacher: bfloat16 [16, 512, 768], P('fsdp', 'tp'), may hold values from -6 to 6
- attn_in: bfloat16 [2, 768, 3, 768], P(None, 'fsdp', None, 'tp'), may hold values from -0.3125 to 0.3125
- attn_out: bfloat16 [2, 768, 768], P(None, 'fsdp', 'tp'), may hold values from -0.625 to 0.625
- ff_in: bfloat16 [2, 768, 3072], P(None, 'fsdp', 'tp'), may hold values from -0.21875 to 0.21875
- ff_out: bfloat16 [2, 768, 3072], P(None, 'fsdp', 'tp'), may hold values from -0.109375 to 0.109375
- biases: bfloat16 [2, 5, 768], P(None, None, 'fsdp'), may hold values from -1.5 to 1.5
- gains: bfloat16 [2, 2, 768], P(None, None, 'fsdp'), may hold values from 0.5 to 1.5
- ff_bias: bfloat16 [2, 3072], P(None, 'fsdp'), may hold values from -1.5 to 1.5
- query_bias: bfloat16 [2, 768], P(None, 'fsdp'), may hold values from -1.5 to 1.5
Outputs:
- mixed: bfloat16 [16, 512, 768], P('fsdp', 'tp')
- tokens_grad: float32 [16, 512, 768], P('fsdp', 'tp')
- loss: float32 [], replicated
- attn_in_grad: float32 [2, 768, 3, 768], P(None, 'fsdp', None, 'tp')
- attn_out_grad: float32 [2, 768, 768], P(None, 'fsdp', 'tp')
- ff_in_grad: float32 [2, 768, 3072], P(None, 'fsdp', 'tp')
- ff_out_grad: float32 [2, 768, 3072], P(None, 'fsdp', 'tp')
- biases_grad: float32 [2, 5, 768], P(None, None, 'fsdp')
- gains_grad: float32 [2, 2, 768], P(None, None, 'fsdp')
- ff_bias_grad: float32 [2, 3072], P(None, 'fsdp')
- query_bias_grad: float32 [2, 768], P(None, 'fsdp')
Inputs may be any that keep to these rules, and one draw needn't show every extreme that they name: `segments`: along each sequence the ids are 1, 2, 3, ... in runs of 200 to 480 tokens (documents), then 0 (padding) to the end; padding is shorter than 480 tokens; some document of the batch has exactly 480 tokens, and some sequence consists of documents of exactly 200 tokens. `valid`: each flag is 1 independently, with a probability that rises linearly from 1/4 in the first sequence to 3/4 in the last.
All inputs are finite; a program needn't handle non-finite values.
Results may differ from a plain program's by a relative error of at most 0.035.
Values may be sent and summed in bfloat16 or wider, within the bound.
A program may use at most 192 MiB of HBM per device.

v0:
```python
import functools

import jax
import jax.numpy as jnp
from jax import lax
from jax.experimental import pallas as pl
from jax.experimental.pallas import tpu as pltpu
from jax.sharding import PartitionSpec as P

HEAD_DIM = 64
MESH = pl.DeviceIdType.MESH
PIECE = 384
CHUNKS = 2
LANES = 128
GROUP = 16
WINDOW = 3
PUMPS = (
    {
        "projected": (4,),
        "attend": ((1, 5), (2, 6)),
        "norm": ((0, 7), (1, 8)),
        "feed own": (9,),
        "feed": ((0, 10),),
        "fed": (11, 12),
        "sent": (13,),
        "kept": (14,),
        "end": ((0, 15), (1, 16)),
    },
    {
        "own projected": (17, 18),
        "projected": (19,),
        "attend": ((2, 20),),
        "norm": ((0, 21), (1, 22)),
        "feed": ((0, 23), (1, 24)),
    },
)
LAG = 2

epsilon = 1e-05
root_half = 0.7071067811865476
inv_root_tau = 0.3989422804014327
masked = -1e30


def product(left, right):
    return lax.dot_general(left, right, (((1,), (0,)), ((), ())), preferred_element_type=jnp.float32)


def product_nt(left, right):
    return lax.dot_general(left, right, (((1,), (1,)), ((), ())), preferred_element_type=jnp.float32)


def norm_stats(total):
    centred = total - jnp.mean(total, axis=-1, keepdims=True)
    inverse = lax.rsqrt(jnp.mean(centred * centred, axis=-1, keepdims=True) + epsilon)
    return centred * inverse, inverse


def norm_back(grad_out, normed, inverse, gain):
    scaled = grad_out * gain
    return inverse * (
        scaled
        - jnp.mean(scaled, axis=-1, keepdims=True)
        - normed * jnp.mean(scaled * normed, axis=-1, keepdims=True)
    )


def step_kernel(
    extra,
    token_total,
    attn_in_ref,
    attn_out_ref,
    ff_in_ref,
    ff_out_ref,
    tokens_ref,
    biases_ref,
    gains_ref,
    ff_bias_ref,
    query_ref,
    teacher_ref,
    valid_ref,
    seg_ref,
    count_in_ref,
    mixed_ref,
    tokens_grad_ref,
    grad_ref,
    sums_ref,
    count_ref,
    mats,
    small_all,
    param,
    ff_shift,
    from_core,
    from_col,
    from_row,
    x_low,
    qkv,
    heads,
    log_sum,
    h_low,
    act,
    slope,
    normed,
    inverse,
    stream,
    out_part,
    in_part,
    own_part,
    d_low,
    d_qkv,
    d_heads,
    mask,
    pair_turn,
    probs_all,
    scores_all,
    turned,
    sums_in,
    count_mine,
    count_theirs,
    small_ref,
    weight_ref,
    z_send,
    z_recv,
    hop_send,
    hop_recv,
    local_sem,
    s_send,
    s_recv,
    x_send,
    x_recv,
    r_send,
    r_recv,
    a_send,
    a_recv,
    c_send,
    c_recv,
):
    pieces = mats.shape[0]
    layers = x_low.shape[0]
    per_layer = pieces // layers
    half_rows = tokens_ref.shape[0]
    width = tokens_ref.shape[1]
    length = 2 * half_rows
    rows = half_rows // CHUNKS
    pairs = PIECE // LANES
    ups = act.shape[3] // PIECE

    spot = lax.axis_index("fsdp") // extra
    rest = lax.axis_index("fsdp") % extra
    t = lax.axis_index("tp")
    z, y, c = spot // 4, (spot // 2) % 2, spot % 2

    def peer(row, col, core):
        return {"fsdp": ((row * 2 + col) * 2 + core) * extra + rest, "tp": t}

    z_peers = [peer((z + step) % 4, y, c) for step in (1, 2, 3)]
    y_peer = peer(z, 1 - y, c)
    c_peer = peer(z, y, 1 - c)
    x_peer = {"fsdp": lax.axis_index("fsdp"), "tp": 1 - t}
    shards = []
    for layer in range(layers):
        shards += [attn_in_ref.at[layer, j] for j in range(3)]
        for source in (attn_out_ref, ff_in_ref, ff_out_ref):
            shards += [
                source.at[layer, :, pl.ds(j * PIECE, PIECE)] for j in range(source.shape[2] // PIECE)
            ]

    def own_copy(piece):
        return pltpu.make_async_copy(shards[piece], mats.at[piece, z, y, c], local_sem.at[piece])

    own_tokens = pltpu.make_async_copy(tokens_ref, x_low.at[0, t], local_sem.at[pieces])
    own_tokens.start()
    for piece in range(pieces):
        own_copy(piece).start()
    everyone = (*z_peers, y_peer, c_peer, x_peer)
    barrier = pltpu.get_barrier_semaphore()
    for other in everyone:
        pl.semaphore_signal(barrier, inc=1, device_id=other, device_id_type=MESH)
    pl.semaphore_wait(barrier, len(everyone))

    def remote(src, dst, send_sem, recv_sem, device):
        return pltpu.make_async_remote_copy(
            src_ref=src,
            dst_ref=dst,
            send_sem=send_sem,
            recv_sem=recv_sem,
            device_id=device,
            device_id_type=MESH,
        )

    def z_copy(piece, step):
        return remote(
            mats.at[piece, z, y, c],
            mats.at[piece, z, y, c],
            z_send.at[piece, step],
            z_recv.at[piece, step],
            z_peers[step],
        )

    def push(piece):
        for step in range(3):
            z_copy(piece, step).start()

    def hop_copy(piece, kind):
        column = 1 - y if kind == 2 else y
        block = mats.at[piece, :, column, c]
        return remote(
            block,
            block,
            hop_send.at[piece, kind],
            hop_recv.at[piece, kind],
            y_peer if kind == 0 else c_peer,
        )

    def small_z(step):
        block = small_all.at[z, y, c]
        return remote(small_ref, block, s_send.at[step], s_recv.at[step], z_peers[step])

    def small_hop(kind):
        column = 1 - y if kind == 2 else y
        block = small_all.at[:, column, c]
        return remote(
            block, block, s_send.at[3 + kind], s_recv.at[3 + kind], y_peer if kind == 0 else c_peer
        )

    def first_half(piece):
        for step in range(3):
            z_copy(piece, step).wait_recv()
        if isinstance(piece, int):
            if piece + WINDOW < pieces:
                push(piece + WINDOW)
        else:
            pl.when(piece + WINDOW < pieces)(lambda: push(piece + WINDOW))
        hop_copy(piece, 0).start()
        hop_copy(piece, 1).start()

    def second_half(piece):
        hop_copy(piece, 0).wait_recv()
        hop_copy(piece, 2).start()

    def advance(step):
        if isinstance(step, int):
            if step < pieces:
                first_half(step)
            if 0 < step <= pieces:
                second_half(step - 1)
        else:
            pl.when(step < pieces)(lambda: first_half(step))
            pl.when(step <= pieces)(lambda: second_half(step - 1))

    def need(first, count=1):
        for piece in range(first, first + count):
            hop_copy(piece, 1).wait_recv()
            hop_copy(piece, 2).wait_recv()

    def chunk_rows(chunk):
        if isinstance(chunk, int):
            return pl.ds(chunk * rows, rows)
        return pl.ds(pl.multiple_of(chunk * rows, rows), rows)

    def give_rows(number, chunk, block):
        place = block.at[t, chunk_rows(chunk)]
        return remote(place, place, x_send.at[number, chunk], x_recv.at[number, chunk], x_peer)

    def give_part(number, chunk):
        return remote(
            out_part.at[chunk_rows(chunk)],
            in_part.at[chunk_rows(chunk)],
            x_send.at[number, chunk],
            x_recv.at[number, chunk],
            x_peer,
        )

    def put_part(number, previous, chunk, value):
        if previous is not None:
            give_part(previous, chunk).wait_send()
        out_part[chunk_rows(chunk)] = value.astype(jnp.bfloat16)
        give_part(number, chunk).start()

    def place_part(index, number, previous, value):
        chunk = index % CHUNKS

        @pl.when(index < CHUNKS)
        def _():
            put_part(number, previous, chunk, value)

        @pl.when(index >= CHUNKS)
        def _():
            own_part[chunk_rows(chunk)] = value

    def core_copy(piece):
        return remote(
            mats.at[piece, :, :, 1 - c],
            from_core.at[piece],
            r_send.at[piece, 0],
            r_recv.at[piece, 0],
            c_peer,
        )

    def col_copy(piece):
        return remote(
            from_core.at[piece, :, 1 - y],
            from_col.at[piece],
            r_send.at[piece, 1],
            r_recv.at[piece, 1],
            y_peer,
        )

    def row_copy(piece, step):
        return remote(
            from_core.at[piece, (z + step + 1) % 4, y],
            from_row.at[piece, step],
            r_send.at[piece, 2 + step],
            r_recv.at[piece, 2 + step],
            z_peers[step],
        )

    def reduce_core(piece):
        core_copy(piece).wait_recv()

        def add_row(row, carry):
            from_core[piece, row] = (
                from_core[piece, row].astype(jnp.float32)
                + mats[piece, row, :, c].astype(jnp.float32)
            ).astype(jnp.bfloat16)
            return carry

        lax.fori_loop(0, 4, add_row, 0)
        col_copy(piece).start()

    def reduce_col(piece):
        col_copy(piece).wait_recv()

        def add_row(row, carry):
            from_core[piece, row, y] = (
                from_core[piece, row, y].astype(jnp.float32) + from_col[piece, row].astype(jnp.float32)
            ).astype(jnp.bfloat16)
            return carry

        lax.fori_loop(0, 4, add_row, 0)
        for step in range(3):
            row_copy(piece, step).start()

    def reduce_row(piece):
        for step in range(3):
            row_copy(piece, step).wait_recv()
        total = from_core[piece, z, y].astype(jnp.float32)
        for step in range(3):
            total = total + from_row[piece, step].astype(jnp.float32)
        grad_ref[piece] = total

    def reduce_step(index):
        if isinstance(index, int):
            if index < pieces:
                reduce_core(pieces - 1 - index)
            if 0 <= index - LAG < pieces:
                reduce_col(pieces - 1 - (index - LAG))
            if 0 <= index - 2 * LAG < pieces:
                reduce_row(pieces - 1 - (index - 2 * LAG))
        else:
            pl.when(index < pieces)(lambda: reduce_core(pieces - 1 - index))
            pl.when((index >= LAG) & (index < pieces + LAG))(
                lambda: reduce_col(pieces - 1 - (index - LAG))
            )
            pl.when(index >= 2 * LAG)(lambda: reduce_row(pieces - 1 - (index - 2 * LAG)))

    def put_grad(piece, value):
        mats[piece] = value.astype(jnp.bfloat16).reshape(mats.shape[1:])
        core_copy(piece).start()

    sum_blocks = ((8, 24), (0, 8))

    def sum_copy(phase, step):
        first, count = sum_blocks[phase]
        part = sums_ref.at[pl.ds(first, count)]
        slot = step if step < 3 else 3 + z
        device = (c_peer, y_peer, x_peer)[step] if step < 3 else z_peers[step - 3]
        return remote(
            part,
            sums_in.at[slot, pl.ds(first, count)],
            a_send.at[phase, step],
            a_recv.at[phase, step],
            device,
        )

    def sum_start(phase, step):
        if step < 3:
            sum_copy(phase, step).start()
            return
        first, count = sum_blocks[phase]
        for k in range(3, 6):
            sum_copy(phase, k).start()
        sums_in[3 + z, pl.ds(first, count)] = sums_ref[pl.ds(first, count)]

    def sum_finish(phase, step):
        first, count = sum_blocks[phase]
        block = pl.ds(first, count)
        if step < 3:
            sum_copy(phase, step).wait()
            sums_ref[block] = sums_ref[block] + sums_in[step, block]
            return
        for k in range(3, 6):
            sum_copy(phase, k).wait()
        sums_ref[block] = (sums_in[3, block] + sums_in[4, block]) + (
            sums_in[5, block] + sums_in[6, block]
        )

    def add_sum(row, value, column=None):
        if column is None:
            sums_ref[pl.ds(row, 1)] += value
        else:
            sums_ref[pl.ds(row, 1), column] += value

    def par(row):
        return param[pl.ds(row, 1)]

    def matrix(piece, count=1):
        parts = [mats[piece + j].reshape(width, PIECE) for j in range(count)]
        return parts[0] if count == 1 else jnp.concatenate(parts, axis=1)

    def turn(source):
        def turn_rows(index, carry):
            half, chunk = index // CHUNKS, index % CHUNKS
            columns = pl.ds(pl.multiple_of(index * rows, LANES), rows)
            turned[:, columns] = source[half, chunk_rows(chunk)].T
            return carry

        lax.fori_loop(0, 2 * CHUNKS, turn_rows, 0)

    own_columns = pl.ds(pl.multiple_of(t * PIECE, LANES), PIECE)

    for piece in range(WINDOW):
        own_copy(piece).wait()
        push(piece)
    for chunk in range(CHUNKS):
        place = x_low.at[0, t, chunk_rows(chunk)]
        remote(
            tokens_ref.at[chunk_rows(chunk)],
            place,
            x_send.at[0, chunk],
            x_recv.at[0, chunk],
            x_peer,
        ).start()
    seg_q = seg_ref[...].astype(jnp.float32)
    half_lanes = pl.ds(pl.multiple_of(t * half_rows, LANES), half_rows)
    counted_rows = valid_ref[...] * (seg_ref[:, half_lanes] > 0).astype(jnp.int32)
    weights = jnp.broadcast_to(counted_rows.astype(jnp.float32), (8, half_rows)).T
    weight_ref[...] = weights[:, :1]
    if count_in_ref is None:
        count_local = jnp.sum(weights[:, :1], axis=0, keepdims=True)
    else:
        count_local = count_in_ref[:1, :1]
    small_ref[...] = jnp.zeros_like(small_ref)
    share = biases_ref.shape[2]
    kinds = biases_ref.shape[0]
    for layer in range(layers):
        for kind in range(kinds):
            line = biases_ref[kind].astype(jnp.float32)[layer : layer + 1]
            small_ref[pl.ds(layer * kinds + kind, 1), pl.ds(0, share)] = line
        small_ref[pl.ds(10 + layer * 2, 2), pl.ds(0, share)] = gains_ref[layer].astype(jnp.float32)
    small_ref[pl.ds(14, layers), pl.ds(0, share)] = query_ref[...].astype(jnp.float32)
    small_ref[pl.ds(16, layers), pl.ds(0, ff_bias_ref.shape[1])] = ff_bias_ref[...].astype(jnp.float32)
    small_ref[pl.ds(18, 6)] = jnp.broadcast_to(count_local, (6, small_ref.shape[1]))
    own_tokens.wait()
    stream[...] = x_low[0, t].astype(jnp.float32)
    small_all[z, y, c] = small_ref[...]
    for step in range(3):
        small_z(step).start()
    for piece in range(WINDOW, pieces):
        own_copy(piece).wait()
    seg_k = jnp.broadcast_to(seg_q, (8, length)).T[:, :1]
    allowed = (seg_k > 0) & ((seg_k == seg_q) | (seg_q == 0))
    mask[...] = jnp.where(allowed, 0.0, masked)
    sums_ref[...] = jnp.zeros_like(sums_ref)
    lane = lax.broadcasted_iota(jnp.int32, (1, LANES), 1)
    low_lanes = lane < HEAD_DIM
    low_sub = lax.broadcasted_iota(jnp.int32, (LANES, 1), 0) < HEAD_DIM

    for step in range(3):
        small_z(step).wait_recv()
    small_hop(0).start()
    small_hop(1).start()
    small_hop(0).wait_recv()
    small_hop(2).start()
    small_hop(1).wait_recv()
    small_hop(2).wait_recv()
    param[...] = jnp.zeros_like(param)
    ff_shift[...] = jnp.zeros_like(ff_shift)
    counted = jnp.zeros((8, LANES), jnp.float32)
    for place in range(GROUP):
        block = small_all[place // 4, (place // 2) % 2, place % 2]
        offset = place * share
        tile = min(offset // LANES * LANES, width - 2 * LANES)
        shifted = block[:16] if offset == tile else pltpu.roll(block[:16], offset - tile, 1)
        param[pl.ds(0, 16), pl.ds(tile, 2 * LANES)] += shifted
        counted = counted + block[16:24, :LANES]
    hidden_share = ff_shift.shape[1] // (GROUP // 2)
    for place in range(GROUP // 2):
        block = small_all[2 * t + place // 4, (place // 2) % 2, place % 2][16:24]
        offset = place * hidden_share
        tile = offset // LANES * LANES
        if offset != tile:
            block = pltpu.roll(block, offset - tile, 1)
        ff_shift[:, pl.ds(tile, 2 * LANES)] += block
    count_mine[...] = counted
    remote(count_mine, count_theirs, c_send.at[0], c_recv.at[0], x_peer).start()

    def split_heads(pair):
        return jnp.concatenate(
            [jnp.where(low_lanes, pair, 0), jnp.where(low_lanes, 0, pair)], axis=0
        ).astype(pair.dtype)

    def merge_heads(turned_pair):
        size = turned_pair.shape[1] // 2
        return jnp.where(low_sub, turned_pair[:, :size], turned_pair[:, size:]).T

    def pair_lanes(pair):
        return pl.ds(pl.multiple_of(pair * LANES, LANES), LANES)

    def pair_rows(layer, which, pair):
        return qkv[layer, which, :, :, pair_lanes(pair)].reshape(length, LANES)

    def half_of(index):
        return jnp.where(index < CHUNKS, 1 - t, t)

    for layer in range(layers):
        base = layer * per_layer
        ex = 4 * layer
        early = layer == 0

        def project(half, first, count, layer=layer, base=base):
            acc = product(x_low[layer, half], matrix(base + first, count))
            for j in range(first, first + count):
                part = acc[:, (j - first) * PIECE : (j - first + 1) * PIECE]
                if j == 0:
                    part = part + param[pl.ds(14 + layer, 1), own_columns]
                if j == 2:
                    part = part + param[pl.ds(layer * 5, 1), own_columns]
                low = part.astype(jnp.bfloat16)
                if j == 0:
                    low = low * jnp.bfloat16(HEAD_DIM**-0.5)
                qkv[layer, j, half] = low

        def pump(slot, index=None, layer=layer):
            steps = PUMPS[layer].get(slot, ())
            if index is None:
                for step in steps:
                    advance(step)
                return
            for place, step in steps:
                pl.when(index == place)(lambda step=step: advance(step))

        if early:
            advance(0)
            for j in range(3):
                advance(j + 1)
                need(base + j)
                project(t, j, 1)
        else:
            need(base, 3)
            project(t, 0, 3)
        pump("own projected")
        for chunk in range(CHUNKS):
            give_rows(ex, chunk, x_low.at[layer]).wait_recv()
        project(1 - t, 0, 3)
        pump("projected")
        for pair in range(pairs):
            pair_turn[pair] = pair_rows(layer, 2, pair).T

        def attend(index, carry, layer=layer, base=base, ex=ex, early=early, pump=pump):
            half, chunk = half_of(index), index % CHUNKS
            where = chunk_rows(chunk)
            columns = pl.ds(pl.multiple_of(half * half_rows + chunk * rows, rows), rows)
            bias = mask[:, columns]
            bias = jnp.concatenate([bias, bias], axis=1)
            pump("attend", index)
            for pair in range(pairs):
                queries = split_heads(qkv[layer, 0, half, where, pair_lanes(pair)])
                scores = product_nt(pair_rows(layer, 1, pair), queries) + bias
                highest = jnp.max(scores, axis=0, keepdims=True)
                exponent = jnp.exp(scores - highest)
                total = jnp.sum(exponent, axis=0, keepdims=True)
                probs = (exponent * (1.0 / total)).astype(jnp.bfloat16)
                log_sum[layer, pair, half, chunk] = highest + jnp.log(total)
                mixed_pair = merge_heads(product(pair_turn[pair], probs))
                heads[layer, half, where, pair_lanes(pair)] = mixed_pair.astype(jnp.bfloat16)
            pl.when(index == 0)(lambda: need(base + 3))
            part = product_nt(heads[layer, half, where], matrix(base + 3))
            place_part(index, ex + 1, None if early else ex - 1, part)
            return carry

        lax.fori_loop(0, 2 * CHUNKS, attend, 0)

        def norm_rows(chunk, carry, layer=layer, ex=ex, pump=pump):
            where = chunk_rows(chunk)
            pump("norm", chunk)
            give_part(ex + 1, chunk).wait_recv()
            total = (
                stream[where] + own_part[where] + in_part[where].astype(jnp.float32) + par(layer * 5 + 1)
            )
            unit, scale = norm_stats(total)
            normed[layer, 0, where] = unit
            inverse[layer, 0, where] = scale
            value = unit * par(10 + layer * 2) + par(layer * 5 + 2)
            stream[where] = value
            h_low[layer, t, where] = value.astype(jnp.bfloat16)
            give_rows(ex + 2, chunk, h_low.at[layer]).start()
            return carry

        lax.fori_loop(0, CHUNKS, norm_rows, 0)

        need(base + 4, 4)

        def feed(half, where, layer=layer, base=base):
            source = h_low[layer, half, where]
            for j in range(0, ups, 2):
                lanes = pl.ds(j * PIECE, 2 * PIECE)
                u = product(source, matrix(base + 4 + j, 2)) + ff_shift[pl.ds(layer, 1), lanes]
                cdf = 0.5 * (1.0 + lax.erf(u * root_half))
                bell = jnp.exp(-0.5 * u * u) * inv_root_tau
                act[layer, half, where, lanes] = (u * cdf).astype(jnp.bfloat16)
                slope[layer, half, where, lanes] = (cdf + u * bell).astype(jnp.bfloat16)

        def feed_peer(chunk, carry, layer=layer, ex=ex, feed=feed, pump=pump):
            pump("feed", chunk)
            give_rows(ex + 2, chunk, h_low.at[layer]).wait_recv()
            feed(1 - t, chunk_rows(chunk))
            return carry

        def down(half, where, layer=layer, base=base):
            return product_nt(act[layer, half, where], matrix(base + 8, ups))

        def down_peer(chunk, carry, down=down, ex=ex):
            put_part(ex + 3, ex + 1, chunk, down(1 - t, chunk_rows(chunk)))
            return carry

        everything = pl.ds(0, half_rows)
        pump("feed own")
        feed(t, everything)
        lax.fori_loop(0, CHUNKS, feed_peer, 0)
        pump("fed")
        need(base + 8, 4)
        lax.fori_loop(0, CHUNKS, down_peer, 0)
        pump("sent")
        own_part[...] = down(t, everything)
        pump("kept")

        if layer == layers - 1:
            remote(count_mine, count_theirs, c_send.at[0], c_recv.at[0], x_peer).wait()
            count_all = (count_mine[...] + count_theirs[...])[2:3, :1]
            count_ref[...] = jnp.broadcast_to(count_all, count_ref.shape)
            loss_scale = token_total / count_all
        def end_rows(chunk, carry, layer=layer, ex=ex, pump=pump):
            where = chunk_rows(chunk)
            give_part(ex + 3, chunk).wait_recv()
            total = (
                stream[where] + own_part[where] + in_part[where].astype(jnp.float32) + par(layer * 5 + 3)
            )
            unit, scale = norm_stats(total)
            normed[layer, 1, where] = unit
            inverse[layer, 1, where] = scale
            value = unit * par(11 + layer * 2) + par(layer * 5 + 4)
            if layer < layers - 1:
                stream[where] = value
                x_low[layer + 1, t, where] = value.astype(jnp.bfloat16)
                give_rows(ex + 4, chunk, x_low.at[layer + 1]).start()
            else:
                mixed_ref[where] = value.astype(jnp.bfloat16)
                deviation = value - teacher_ref[where].astype(jnp.float32)
                weighted = weight_ref[where] * deviation
                add_sum(24, jnp.sum(weighted * deviation, axis=0, keepdims=True))
                stream[where] = loss_scale * weighted
            pump("end", chunk)
            return carry

        lax.fori_loop(0, CHUNKS, end_rows, 0)

    def finish_gather(piece, carry):
        for k in range(3):
            z_copy(piece, k).wait_send()
            hop_copy(piece, k).wait_send()
        return carry

    lax.fori_loop(0, pieces, finish_gather, 0)

    for layer in range(layers - 1, -1, -1):
        base = layer * per_layer
        ex = 4 * layers + 4 * (layers - 1 - layer)
        last = layer == layers - 1
        done = 0 if last else per_layer
        sums_base = layer * 8

        def top_rows(chunk, carry, layer=layer, ex=ex, last=last, sums_base=sums_base):
            where = chunk_rows(chunk)
            if not last:
                give_part(ex - 1, chunk).wait_recv()
                stream[where] += own_part[where] + in_part[where].astype(jnp.float32)
            grad_out, unit = stream[where], normed[layer, 1, where]
            below = norm_back(grad_out, unit, inverse[layer, 1, where], par(11 + layer * 2))
            d_low[layer, 0, t, where] = below.astype(jnp.bfloat16)
            give_rows(ex, chunk, d_low.at[layer, 0]).start()
            stream[where] = below
            add_sum(sums_base + 6, jnp.sum(grad_out * unit, axis=0, keepdims=True))
            add_sum(sums_base + 4, jnp.sum(grad_out, axis=0, keepdims=True))
            add_sum(sums_base + 3, jnp.sum(below, axis=0, keepdims=True))
            return carry

        lax.fori_loop(0, CHUNKS, top_rows, 0)
        if not last:
            reduce_step(9)

        def feed_back(half, where, layer=layer, base=base):
            source = d_low[layer, 0, half, where]
            per_row = width // PIECE
            for j in range(0, ups, 2):
                lanes = pl.ds(j * PIECE, 2 * PIECE)
                du = product(source, matrix(base + 8 + j, 2)) * slope[
                    layer, half, where, lanes
                ].astype(jnp.float32)
                total = jnp.sum(du, axis=0, keepdims=True)
                for k in range(j, j + 2):
                    add_sum(
                        16 + layer * 4 + 2 * t + k // per_row,
                        total[:, (k - j) * PIECE : (k - j + 1) * PIECE],
                        pl.ds(k % per_row * PIECE, PIECE),
                    )
                slope[layer, half, where, lanes] = du.astype(jnp.bfloat16)

        def up_back(half, where, layer=layer, base=base):
            return product_nt(slope[layer, half, where], matrix(base + 4, ups))

        def feed_back_peer(chunk, carry, layer=layer, ex=ex, last=last, feed_back=feed_back, up_back=up_back):
            if not last:
                reduce_step(10 + chunk)
            where = chunk_rows(chunk)
            give_rows(ex, chunk, d_low.at[layer, 0]).wait_recv()
            feed_back(1 - t, where)
            put_part(ex + 1, 4 * layers - 1 if last else ex - 1, chunk, up_back(1 - t, where))
            return carry

        feed_back(t, everything)
        lax.fori_loop(0, CHUNKS, feed_back_peer, 0)

        def mid_rows(chunk, layer=layer, ex=ex, sums_base=sums_base):
            where = chunk_rows(chunk)
            give_part(ex + 1, chunk).wait_recv()
            grad_out = stream[where] + own_part[where] + in_part[where].astype(jnp.float32)
            unit = normed[layer, 0, where]
            below = norm_back(grad_out, unit, inverse[layer, 0, where], par(10 + layer * 2))
            d_low[layer, 1, t, where] = below.astype(jnp.bfloat16)
            give_rows(ex + 2, chunk, d_low.at[layer, 1]).start()
            stream[where] = below
            add_sum(sums_base + 5, jnp.sum(grad_out * unit, axis=0, keepdims=True))
            add_sum(sums_base + 2, jnp.sum(grad_out, axis=0, keepdims=True))
            add_sum(sums_base + 1, jnp.sum(below, axis=0, keepdims=True))

        def pair_grad(piece, left, right, j):
            lanes = pl.ds(j * PIECE, 2 * PIECE)
            if not isinstance(j, int):
                lanes = pl.ds(pl.multiple_of(j * PIECE, LANES), 2 * PIECE)
            both = product(left, right[:, :, lanes].reshape(length, 2 * PIECE))
            put_grad(piece + 1, both[:, PIECE:])
            put_grad(piece, both[:, :PIECE])

        def up_grad(j, layer=layer, base=base, pair_grad=pair_grad):
            pair_grad(base + 4 + j, turned[...], slope.at[layer], j)

        turn(d_low.at[layer, 0])

        def down_grads(index, carry, layer=layer, base=base, pair_grad=pair_grad):
            j = ups - 2 - 2 * index
            pair_grad(base + 8 + j, turned[...], act.at[layer], j)
            return carry

        lax.fori_loop(0, ups // 2, down_grads, 0)
        if not last:
            sum_start(0, 0)
        own_part[...] = up_back(t, everything)
        mid_rows(0)
        reduce_step(done)
        if not last:
            sum_finish(0, 0)
            sum_start(0, 1)
        turn(h_low.at[layer])
        up_grad(ups - 2)
        mid_rows(1)
        reduce_step(done + 1)
        if not last:
            sum_finish(0, 1)
            sum_start(0, 2)
        for j in range(ups - 4, -1, -2):
            up_grad(j)
        d_heads[t] = product(d_low[layer, 1, t], matrix(base + 3)).astype(jnp.bfloat16)
        for pair in range(pairs):
            pair_turn[pair] = pair_rows(layer, 1, pair).T
        reduce_step(done + 2)
        if not last:
            sum_finish(0, 2)
            sum_start(0, 3)
        reduce_step(done + 3)
        for chunk in range(CHUNKS):
            give_rows(ex + 2, chunk, d_low.at[layer, 1]).wait_recv()
        d_heads[1 - t] = product(d_low[layer, 1, 1 - t], matrix(base + 3)).astype(jnp.bfloat16)

        def pair_back(pair, carry, layer=layer, done=done):
            lanes = pair_lanes(pair)
            keys_in, values_in = pair_rows(layer, 1, pair), pair_rows(layer, 2, pair)

            def attend_back(index, carry, layer=layer, pair=pair, lanes=lanes, done=done):
                spent = pair * 2 * CHUNKS + index
                pl.when(spent % 3 == 2)(lambda: reduce_step(done + 4 + spent // 3))
                half, chunk = index // CHUNKS, index % CHUNKS
                where = chunk_rows(chunk)
                columns = pl.ds(pl.multiple_of(index * rows, rows), rows)
                bias = mask[:, columns]
                bias = jnp.concatenate([bias, bias], axis=1)
                keys_in, values_in = pair_rows(layer, 1, pair), pair_rows(layer, 2, pair)
                queries = split_heads(qkv[layer, 0, half, where, lanes])
                grads = split_heads(d_heads[half, where, lanes])
                scores = product_nt(keys_in, queries) + bias
                probs = jnp.exp(scores - log_sum[layer, pair, half, chunk])
                d_probs = product_nt(values_in, grads)
                delta = jnp.sum(probs * d_probs, axis=0, keepdims=True)
                d_scores = (probs * (d_probs - delta)).astype(jnp.bfloat16)
                double = pl.ds(pl.multiple_of(index * 2 * rows, LANES), 2 * rows)
                probs_all[:, double] = probs.astype(jnp.bfloat16)
                scores_all[:, double] = d_scores
                d_query = merge_heads(product(pair_turn[pair], d_scores)) * HEAD_DIM**-0.5
                d_qkv[0, half, where, lanes] = d_query.astype(jnp.bfloat16)
                return carry

            lax.fori_loop(0, 2 * CHUNKS, attend_back, 0)
            query_list, grad_list = [], []
            for index in range(2 * CHUNKS):
                half, where = index // CHUNKS, chunk_rows(index % CHUNKS)
                query_list.append(split_heads(qkv[layer, 0, half, where, lanes]))
                grad_list.append(split_heads(d_heads[half, where, lanes]))
            d_keys = product(scores_all[...], jnp.concatenate(query_list, axis=0))
            d_values = product(probs_all[...], jnp.concatenate(grad_list, axis=0))
            d_qkv[1, :, :, lanes] = d_keys.astype(jnp.bfloat16).reshape(2, half_rows, LANES)
            d_qkv[2, :, :, lanes] = d_values.astype(jnp.bfloat16).reshape(2, half_rows, LANES)
            return carry

        lax.fori_loop(0, pairs, pair_back, 0)

        def query_parts(index, carry, layer=layer, base=base, ex=ex):
            half, chunk = half_of(index), index % CHUNKS
            where = chunk_rows(chunk)
            parts = jnp.concatenate([d_qkv[j, half, where] for j in range(3)], axis=1)
            part = product_nt(parts, matrix(base, 3))
            place_part(index, ex + 3, ex + 1, part)
            return carry

        add_sum(
            sums_base + 7,
            jnp.sum(d_qkv[0].reshape(length, PIECE).astype(jnp.float32), axis=0, keepdims=True),
            own_columns,
        )
        add_sum(
            sums_base,
            jnp.sum(d_qkv[2].reshape(length, PIECE).astype(jnp.float32), axis=0, keepdims=True),
            own_columns,
        )
        if not last:
            sum_start(1, 0)
        lax.fori_loop(0, 2 * CHUNKS, query_parts, 0)
        turn(d_low.at[layer, 1])
        put_grad(base + 3, product(turned[...], heads[layer].reshape(length, PIECE)))
        turn(x_low.at[layer])
        for j in range(2, -1, -1):
            put_grad(base + j, product(turned[...], d_qkv[j].reshape(length, PIECE)))
        reduce_step(done + 8)

    sum_finish(1, 0)
    sum_start(1, 1)
    ex = 8 * layers - 1
    for chunk in range(CHUNKS):
        where = chunk_rows(chunk)
        give_part(ex, chunk).wait_recv()
        tokens_grad_ref[where] = stream[where] + own_part[where] + in_part[where].astype(jnp.float32)
    sum_finish(0, 3)
    sum_finish(1, 1)
    sum_start(1, 2)
    reduce_step(pieces - 3)
    sum_finish(1, 2)
    sum_start(1, 3)

    def drain(step, carry):
        reduce_step(step)
        return carry

    lax.fori_loop(pieces - 2, pieces + 2 * LAG, drain, 0)
    sum_finish(1, 3)

    for step in range(3):
        small_z(step).wait_send()
        small_hop(step).wait_send()
    for chunk in range(CHUNKS):
        give_part(8 * layers - 1, chunk).wait_send()
        for layer in range(layers):
            give_rows(4 * layer, chunk, x_low.at[layer]).wait_send()
            give_rows(4 * layer + 2, chunk, h_low.at[layer]).wait_send()
            number = 4 * layers + 4 * (layers - 1 - layer)
            give_rows(number, chunk, d_low.at[layer, 0]).wait_send()
            give_rows(number + 2, chunk, d_low.at[layer, 1]).wait_send()

    def finish_grads(piece, carry):
        core_copy(piece).wait_send()
        col_copy(piece).wait_send()
        for step in range(3):
            row_copy(piece, step).wait_send()
        return carry

    lax.fori_loop(0, pieces, finish_grads, 0)


def run_step(extra, token_total, matrices, vectors, tokens, teacher, valid, seg_ids, counted):
    attn_in, attn_out, ff_in, ff_out = matrices
    rows, width = tokens.shape
    length = 2 * rows
    layers, share, hidden_width = ff_in.shape
    ups = hidden_width // PIECE
    pieces = layers * (4 + 2 * ups)
    low, full = jnp.bfloat16, jnp.float32
    chunk = rows // CHUNKS
    pairs = PIECE // LANES
    blocks = (4, 2, 2, share, PIECE)
    dma = pltpu.SemaphoreType.DMA
    vmem = pl.BlockSpec(memory_space=pltpu.VMEM)
    operands = [*matrices, tokens, *vectors, teacher, valid, seg_ids]
    kernel = functools.partial(step_kernel, extra, token_total)
    if counted is None:
        inputs = len(operands)

        def body(*refs):
            kernel(*refs[:inputs], None, *refs[inputs:])

    else:
        operands.append(counted)
        body = kernel
    return pl.pallas_call(
        body,
        out_shape=(
            jax.ShapeDtypeStruct((rows, width), low),
            jax.ShapeDtypeStruct((rows, width), full),
            jax.ShapeDtypeStruct((pieces, share, PIECE), full),
            jax.ShapeDtypeStruct((32, width), full),
            jax.ShapeDtypeStruct((8, LANES), full),
        ),
        in_specs=[pl.BlockSpec(memory_space=pl.ANY)] * 5 + [vmem] * (len(operands) - 5),
        out_specs=(vmem,) * 5,
        scratch_shapes=[
            pltpu.VMEM((pieces, *blocks), low),
            pltpu.VMEM((4, 2, 2, 24, 2 * LANES), full),
            pltpu.VMEM((16, width), full),
            pltpu.VMEM((8, hidden_width), full),
            pltpu.VMEM((pieces, 4, 2, share, PIECE), low),
            pltpu.VMEM((pieces, 4, share, PIECE), low),
            pltpu.VMEM((pieces, 3, share, PIECE), low),
            pltpu.VMEM((layers, 2, rows, width), low),
            pltpu.VMEM((layers, 3, 2, rows, PIECE), low),
            pltpu.VMEM((layers, 2, rows, PIECE), low),
            pltpu.VMEM((layers, pairs, 2, CHUNKS, 1, 2 * chunk), full),
            pltpu.VMEM((layers, 2, rows, width), low),
            pltpu.VMEM((layers, 2, rows, hidden_width), low),
            pltpu.VMEM((layers, 2, rows, hidden_width), low),
            pltpu.VMEM((layers, 2, rows, width), full),
            pltpu.VMEM((layers, 2, rows, 1), full),
            pltpu.VMEM((rows, width), full),
            pltpu.VMEM((rows, width), low),
            pltpu.VMEM((rows, width), low),
            pltpu.VMEM((rows, width), full),
            pltpu.VMEM((layers, 2, 2, rows, width), low),
            pltpu.VMEM((3, 2, rows, PIECE), low),
            pltpu.VMEM((2, rows, PIECE), low),
            pltpu.VMEM((length, length), full),
            pltpu.VMEM((pairs, LANES, length), low),
            pltpu.VMEM((length, 2 * length), low),
            pltpu.VMEM((length, 2 * length), low),
            pltpu.VMEM((width, length), low),
            pltpu.VMEM((7, 32, width), full),
            pltpu.VMEM((8, LANES), full),
            pltpu.VMEM((8, LANES), full),
            pltpu.VMEM((24, 2 * LANES), full),
            pltpu.VMEM((rows, 1), full),
            dma((pieces, 3)),
            dma((pieces, 3)),
            dma((pieces, 3)),
            dma((pieces, 3)),
            dma((pieces + 1,)),
            dma((6,)),
            dma((6,)),
            dma((8 * layers, CHUNKS)),
            dma((8 * layers, CHUNKS)),
            dma((pieces, 5)),
            dma((pieces, 5)),
            dma((2, 6)),
            dma((2, 6)),
            dma((1,)),
            dma((1,)),
        ],
        compiler_params=pltpu.CompilerParams(
            collective_id=0, has_side_effects=True, vmem_limit_bytes=67_043_328
        ),
        name="encoder_step",
    )(*operands)


def sibling_groups(extra):
    size = lax.axis_size("fsdp")
    return [list(range(first, first + extra)) for first in range(0, size, extra)]


def widen(shard, extra, axis):
    if extra == 1:
        return shard
    return lax.all_gather(
        shard, "fsdp", axis=axis, axis_index_groups=sibling_groups(extra), tiled=True
    )


def sum_siblings(value, extra):
    if extra == 1:
        return value
    return lax.psum(value, "fsdp", axis_index_groups=sibling_groups(extra))


def finish_kernel(
    place_count,
    mixed_hbm,
    tokens_grad_hbm,
    grad_hbm,
    sums_hbm,
    count_hbm,
    mixed_out,
    tokens_grad_out,
    loss_out,
    attn_in_out,
    attn_out_out,
    ff_in_out,
    ff_out_out,
    biases_out,
    gains_out,
    ff_bias_out,
    query_out,
    sums_ref,
    count_ref,
    sem,
):
    layers = attn_in_out.shape[0]
    width = sums_ref.shape[1]
    per_layer = grad_hbm.shape[0] // layers
    ups = (per_layer - 4) // 2
    moves = [
        (sums_hbm, sums_ref),
        (count_hbm, count_ref),
        (mixed_hbm, mixed_out),
        (tokens_grad_hbm, tokens_grad_out),
    ]
    for layer in range(layers):
        base = layer * per_layer
        for j in range(3):
            moves.append((grad_hbm.at[base + j], attn_in_out.at[layer, j]))
        moves.append((grad_hbm.at[base + 3], attn_out_out.at[layer]))
        for j in range(ups):
            lanes = pl.ds(j * PIECE, PIECE)
            moves.append((grad_hbm.at[base + 4 + j], ff_in_out.at[layer, :, lanes]))
            moves.append((grad_hbm.at[base + 4 + ups + j], ff_out_out.at[layer, :, lanes]))
    copies = [
        pltpu.make_async_copy(source, target, sem.at[number])
        for number, (source, target) in enumerate(moves)
    ]
    for copy in copies:
        copy.start()
    copies[0].wait()
    copies[1].wait()
    squares = jnp.sum(sums_ref[pl.ds(24, 1)], axis=1, keepdims=True)
    loss_out[...] = squares / (count_ref[:1, :1] * width)
    place = lax.axis_index("fsdp")
    share = width // place_count
    own = pltpu.roll(sums_ref[:16], (width - place * share) % width, 1)[:, :share]
    up_share = ff_bias_out.shape[1]
    first = place * up_share
    for layer in range(layers):
        for kind in range(biases_out.shape[0]):
            biases_out[kind, pl.ds(layer, 1)] = own[layer * 8 + kind : layer * 8 + kind + 1]
        gains_out[layer] = own[layer * 8 + 5 : layer * 8 + 7]
        query_out[pl.ds(layer, 1)] = own[layer * 8 + 7 : layer * 8 + 8]
        row = jnp.broadcast_to(sums_ref[pl.ds(16 + layer * 4 + first // width, 1)], (8, width))
        ff_bias_out[pl.ds(layer, 1)] = pltpu.roll(row, (width - first % width) % width, 1)[:1, :up_share]
    for copy in copies[2:]:
        copy.wait()


def on_device(
    tokens,
    segments,
    valid,
    teacher,
    attn_in,
    attn_out,
    ff_in,
    ff_out,
    biases,
    gains,
    ff_bias,
    query_bias,
):
    size = lax.axis_size("fsdp")
    extra = size // GROUP
    layers = attn_in.shape[0]
    rows_dev, width = tokens.shape[1], tokens.shape[2]
    length = segments.shape[1]

    matrices = (
        jnp.swapaxes(widen(attn_in, extra, 1), 1, 2),
        widen(attn_out, extra, 1),
        widen(ff_in, extra, 1),
        widen(ff_out, extra, 1),
    )
    vectors = (
        jnp.swapaxes(widen(biases, extra, 2), 0, 1),
        widen(gains, extra, 2),
        widen(ff_bias, extra, 1),
        widen(query_bias, extra, 1),
    )
    counted = None
    if extra > 1:
        own_seg = lax.dynamic_slice_in_dim(segments, lax.axis_index("tp") * rows_dev, rows_dev, 1)
        total = sum_siblings(jnp.sum((valid * (own_seg > 0)).astype(jnp.float32)), extra)
        counted = jnp.broadcast_to(total, (8, LANES))
    mixed, tokens_grad, grads, sums, count = run_step(
        extra,
        float(length * size),
        matrices,
        vectors,
        tokens[0],
        teacher[0],
        valid,
        segments,
        counted,
    )
    if extra > 1:
        grads = lax.psum_scatter(
            grads, "fsdp", scatter_dimension=1, axis_index_groups=sibling_groups(extra), tiled=True
        )
        sums = sum_siblings(sums, extra)
    vmem = pl.BlockSpec(memory_space=pltpu.VMEM)
    full = jnp.float32
    shapes = [
        jax.ShapeDtypeStruct(mixed.shape, jnp.bfloat16),
        jax.ShapeDtypeStruct(tokens_grad.shape, full),
        jax.ShapeDtypeStruct((1, 1), full),
    ]
    turned_in = (layers, 3, attn_in.shape[1], PIECE)
    turned_biases = (biases.shape[1], layers, biases.shape[2])
    for shape in (turned_in, attn_out.shape, ff_in.shape, ff_out.shape, turned_biases):
        shapes.append(jax.ShapeDtypeStruct(shape, full))
    for part in (gains, ff_bias, query_bias):
        shapes.append(jax.ShapeDtypeStruct(part.shape, full))
    mixed, tokens_grad, loss, in_grad, out_grad, up_grad, down_grad, bias_grad, *rest = pl.pallas_call(
        functools.partial(finish_kernel, size),
        out_shape=tuple(shapes),
        in_specs=[pl.BlockSpec(memory_space=pltpu.HBM)] * 5,
        out_specs=(vmem,) * len(shapes),
        scratch_shapes=[
            pltpu.VMEM(sums.shape, full),
            pltpu.VMEM(count.shape, full),
            pltpu.SemaphoreType.DMA((4 + grads.shape[0],)),
        ],
        compiler_params=pltpu.CompilerParams(vmem_limit_bytes=24 * 1024 * 1024),
        name="place_results",
    )(mixed, tokens_grad, grads, sums, count)
    return (
        mixed[None],
        tokens_grad[None],
        loss[0, 0],
        jnp.swapaxes(in_grad, 1, 2),
        out_grad,
        up_grad,
        down_grad,
        jnp.swapaxes(bias_grad, 0, 1),
        *rest,
    )


def solution(mesh):
    in_specs = (
        P("fsdp", "tp", None),
        P("fsdp", None),
        P("fsdp", "tp"),
        P("fsdp", "tp", None),
        P(None, "fsdp", None, "tp"),
        P(None, "fsdp", "tp"),
        P(None, "fsdp", "tp"),
        P(None, "fsdp", "tp"),
        P(None, None, "fsdp"),
        P(None, None, "fsdp"),
        P(None, "fsdp"),
        P(None, "fsdp"),
    )
    out_specs = (
        P("fsdp", "tp", None),
        P("fsdp", "tp", None),
        P(),
        P(None, "fsdp", None, "tp"),
        P(None, "fsdp", "tp"),
        P(None, "fsdp", "tp"),
        P(None, "fsdp", "tp"),
        P(None, None, "fsdp"),
        P(None, None, "fsdp"),
        P(None, "fsdp"),
        P(None, "fsdp"),
    )
    return jax.shard_map(
        on_device, mesh=mesh, in_specs=in_specs, out_specs=out_specs, check_vma=False
    )
```

profile of v0, /device:TPU:0, one launch (start us, length us, event | category | flops | bytes accessed | tf_op | source)
XLA Modules:
  0.0 272.5 jit_solution(6218533663923983744)
XLA Ops:
  0.6 263.1 %encoder_step.1 = (bf16[256,768]{1,0:T(8,128)(2,1)}, f32[256,768]{1,0:T(8,128)}, f32[24,48,384]{2,1,0:T(8,128)}, f32[32,768]{1,0:T(8,128)}, f32[8,128]{1,0:T(8,128)}) custom-call(bf16[2,3,48,384]{3,2,1,0:T(8,128)(2,1)} %bitcast.11, bf16[2,48,384]{2,1,0:T(8,128)(2,1)} %refs_1_.1, bf16[2,48,1536]{2,1,0:T(8,128)(2,1)} %refs_2_.1, bf16[2,48,1536]{2,1,0:T(8,128)(2,1)} %refs_3_.1, ...), custom_call_target="tpu_custom_call" | custom-call | tf_op jit(solution)/shard_map/encoder_step/pallas_call | solution.py:941
  263.7 0.0 copy-start
  263.7 1.5 copy-done
  265.2 0.0 copy-start.1
  265.2 1.1 copy-done.1
  266.3 0.0 copy-start.2
  266.3 1.0 copy-done.2
  267.3 0.0 copy-start.3
  267.3 0.9 copy-done.3
  268.2 0.0 copy-start.4
  268.2 0.7 copy-done.4
  268.9 3.4 %place_results.1 = (bf16[256,768]{1,0:T(8,128)(2,1)}, f32[256,768]{1,0:T(8,128)}, f32[1,1]{1,0:T(1,128)}, f32[2,3,48,384]{3,2,1,0:T(8,128)}, f32[2,48,384]{2,1,0...) custom-call(bf16[256,768]{1,0:T(8,128)(2,1)S(1)} %copy-done.2, ...), custom_call_target="tpu_custom_call" | custom-call | tf_op jit(solution)/shard_map/place_results/pallas_call | solution.py:1161
Async XLA Ops:
  263.7 1.5 copy-start
  265.2 1.1 copy-start.1
  266.3 1.0 copy-start.2
  267.3 0.9 copy-start.3
  268.2 0.7 copy-start.4
where the time goes:
time: 273 us
  Pallas kernels  266 us (97%)
  local copies, waits for them, and re-layouts  5.16 us (2%)
    pallas_call x1, Pallas kernels, run_step(): pl.pallas_call(body, out_shape=(jax.ShapeDtypeStruct((rows, width), low),...  263 us

commit v1 on v0

--- a/solution.py
+++ b/solution.py
@@ -14,6 +14,8 @@
 LANES = 128
 GROUP = 16
 WINDOW = 3
+ROW_LEAD = 2
+COL_LEAD = 1
 PUMPS = (
     {
         "projected": (4,),
@@ -65,6 +67,11 @@
     )
 
 
+def places(grad_rows, rows):
+    first = grad_rows
+    return first, first + 2 * rows, first + 4 * rows, first + 4 * rows + 64, first + 4 * rows + 72
+
+
 def step_kernel(
     extra,
     token_total,
@@ -81,11 +88,7 @@
     valid_ref,
     seg_ref,
     count_in_ref,
-    mixed_ref,
-    tokens_grad_ref,
-    grad_ref,
-    sums_ref,
-    count_ref,
+    out_ref,
     mats,
     small_all,
     param,
@@ -113,8 +116,10 @@
     pair_turn,
     probs_all,
     scores_all,
+    pair_sums,
     turned,
     sums_in,
+    sums_ref,
     count_mine,
     count_theirs,
     small_ref,
@@ -136,6 +141,7 @@
     c_recv,
 ):
     pieces = mats.shape[0]
+    spots = places(pieces * mats.shape[4], teacher_ref.shape[0])
     layers = x_low.shape[0]
     per_layer = pieces // layers
     half_rows = tokens_ref.shape[0]
@@ -176,271 +182,6 @@
     barrier = pltpu.get_barrier_semaphore()
     for other in everyone:
         pl.semaphore_signal(barrier, inc=1, device_id=other, device_id_type=MESH)
-    pl.semaphore_wait(barrier, len(everyone))
-
-    def remote(src, dst, send_sem, recv_sem, device):
-        return pltpu.make_async_remote_copy(
-            src_ref=src,
-            dst_ref=dst,
-            send_sem=send_sem,
-            recv_sem=recv_sem,
-            device_id=device,
-            device_id_type=MESH,
-        )
-
-    def z_copy(piece, step):
-        return remote(
-            mats.at[piece, z, y, c],
-            mats.at[piece, z, y, c],
-            z_send.at[piece, step],
-            z_recv.at[piece, step],
-            z_peers[step],
-        )
-
-    def push(piece):
-        for step in range(3):
-            z_copy(piece, step).start()
-
-    def hop_copy(piece, kind):
-        column = 1 - y if kind == 2 else y
-        block = mats.at[piece, :, column, c]
-        return remote(
-            block,
-            block,
-            hop_send.at[piece, kind],
-            hop_recv.at[piece, kind],
-            y_peer if kind == 0 else c_peer,
-        )
-
-    def small_z(step):
-        block = small_all.at[z, y, c]
-        return remote(small_ref, block, s_send.at[step], s_recv.at[step], z_peers[step])
-
-    def small_hop(kind):
-        column = 1 - y if kind == 2 else y
-        block = small_all.at[:, column, c]
-        return remote(
-            block, block, s_send.at[3 + kind], s_recv.at[3 + kind], y_peer if kind == 0 else c_peer
-        )
-
-    def first_half(piece):
-        for step in range(3):
-            z_copy(piece, step).wait_recv()
-        if isinstance(piece, int):
-            if piece + WINDOW < pieces:
-                push(piece + WINDOW)
-        else:
-            pl.when(piece + WINDOW < pieces)(lambda: push(piece + WINDOW))
-        hop_copy(piece, 0).start()
-        hop_copy(piece, 1).start()
-
-    def second_half(piece):
-        hop_copy(piece, 0).wait_recv()
-        hop_copy(piece, 2).start()
-
-    def advance(step):
-        if isinstance(step, int):
-            if step < pieces:
-                first_half(step)
-            if 0 < step <= pieces:
-                second_half(step - 1)
-        else:
-            pl.when(step < pieces)(lambda: first_half(step))
-            pl.when(step <= pieces)(lambda: second_half(step - 1))
-
-    def need(first, count=1):
-        for piece in range(first, first + count):
-            hop_copy(piece, 1).wait_recv()
-            hop_copy(piece, 2).wait_recv()
-
-    def chunk_rows(chunk):
-        if isinstance(chunk, int):
-            return pl.ds(chunk * rows, rows)
-        return pl.ds(pl.multiple_of(chunk * rows, rows), rows)
-
-    def give_rows(number, chunk, block):
-        place = block.at[t, chunk_rows(chunk)]
-        return remote(place, place, x_send.at[number, chunk], x_recv.at[number, chunk], x_peer)
-
-    def give_part(number, chunk):
-        return remote(
-            out_part.at[chunk_rows(chunk)],
-            in_part.at[chunk_rows(chunk)],
-            x_send.at[number, chunk],
-            x_recv.at[number, chunk],
-            x_peer,
-        )
-
-    def put_part(number, previous, chunk, value):
-        if previous is not None:
-            give_part(previous, chunk).wait_send()
-        out_part[chunk_rows(chunk)] = value.astype(jnp.bfloat16)
-        give_part(number, chunk).start()
-
-    def place_part(index, number, previous, value):
-        chunk = index % CHUNKS
-
-        @pl.when(index < CHUNKS)
-        def _():
-            put_part(number, previous, chunk, value)
-
-        @pl.when(index >= CHUNKS)
-        def _():
-            own_part[chunk_rows(chunk)] = value
-
-    def core_copy(piece):
-        return remote(
-            mats.at[piece, :, :, 1 - c],
-            from_core.at[piece],
-            r_send.at[piece, 0],
-            r_recv.at[piece, 0],
-            c_peer,
-        )
-
-    def col_copy(piece):
-        return remote(
-            from_core.at[piece, :, 1 - y],
-            from_col.at[piece],
-            r_send.at[piece, 1],
-            r_recv.at[piece, 1],
-            y_peer,
-        )
-
-    def row_copy(piece, step):
-        return remote(
-            from_core.at[piece, (z + step + 1) % 4, y],
-            from_row.at[piece, step],
-            r_send.at[piece, 2 + step],
-            r_recv.at[piece, 2 + step],
-            z_peers[step],
-        )
-
-    def reduce_core(piece):
-        core_copy(piece).wait_recv()
-
-        def add_row(row, carry):
-            from_core[piece, row] = (
-                from_core[piece, row].astype(jnp.float32)
-                + mats[piece, row, :, c].astype(jnp.float32)
-            ).astype(jnp.bfloat16)
-            return carry
-
-        lax.fori_loop(0, 4, add_row, 0)
-        col_copy(piece).start()
-
-    def reduce_col(piece):
-        col_copy(piece).wait_recv()
-
-        def add_row(row, carry):
-            from_core[piece, row, y] = (
-                from_core[piece, row, y].astype(jnp.float32) + from_col[piece, row].astype(jnp.float32)
-            ).astype(jnp.bfloat16)
-            return carry
-
-        lax.fori_loop(0, 4, add_row, 0)
-        for step in range(3):
-            row_copy(piece, step).start()
-
-    def reduce_row(piece):
-        for step in range(3):
-            row_copy(piece, step).wait_recv()
-        total = from_core[piece, z, y].astype(jnp.float32)
-        for step in range(3):
-            total = total + from_row[piece, step].astype(jnp.float32)
-        grad_ref[piece] = total
-
-    def reduce_step(index):
-        if isinstance(index, int):
-            if index < pieces:
-                reduce_core(pieces - 1 - index)
-            if 0 <= index - LAG < pieces:
-                reduce_col(pieces - 1 - (index - LAG))
-            if 0 <= index - 2 * LAG < pieces:
-                reduce_row(pieces - 1 - (index - 2 * LAG))
-        else:
-            pl.when(index < pieces)(lambda: reduce_core(pieces - 1 - index))
-            pl.when((index >= LAG) & (index < pieces + LAG))(
-                lambda: reduce_col(pieces - 1 - (index - LAG))
-            )
-            pl.when(index >= 2 * LAG)(lambda: reduce_row(pieces - 1 - (index - 2 * LAG)))
-
-    def put_grad(piece, value):
-        mats[piece] = value.astype(jnp.bfloat16).reshape(mats.shape[1:])
-        core_copy(piece).start()
-
-    sum_blocks = ((8, 24), (0, 8))
-
-    def sum_copy(phase, step):
-        first, count = sum_blocks[phase]
-        part = sums_ref.at[pl.ds(first, count)]
-        slot = step if step < 3 else 3 + z
-        device = (c_peer, y_peer, x_peer)[step] if step < 3 else z_peers[step - 3]
-        return remote(
-            part,
-            sums_in.at[slot, pl.ds(first, count)],
-            a_send.at[phase, step],
-            a_recv.at[phase, step],
-            device,
-        )
-
-    def sum_start(phase, step):
-        if step < 3:
-            sum_copy(phase, step).start()
-            return
-        first, count = sum_blocks[phase]
-        for k in range(3, 6):
-            sum_copy(phase, k).start()
-        sums_in[3 + z, pl.ds(first, count)] = sums_ref[pl.ds(first, count)]
-
-    def sum_finish(phase, step):
-        first, count = sum_blocks[phase]
-        block = pl.ds(first, count)
-        if step < 3:
-            sum_copy(phase, step).wait()
-            sums_ref[block] = sums_ref[block] + sums_in[step, block]
-            return
-        for k in range(3, 6):
-            sum_copy(phase, k).wait()
-        sums_ref[block] = (sums_in[3, block] + sums_in[4, block]) + (
-            sums_in[5, block] + sums_in[6, block]
-        )
-
-    def add_sum(row, value, column=None):
-        if column is None:
-            sums_ref[pl.ds(row, 1)] += value
-        else:
-            sums_ref[pl.ds(row, 1), column] += value
-
-    def par(row):
-        return param[pl.ds(row, 1)]
-
-    def matrix(piece, count=1):
-        parts = [mats[piece + j].reshape(width, PIECE) for j in range(count)]
-        return parts[0] if count == 1 else jnp.concatenate(parts, axis=1)
-
-    def turn(source):
-        def turn_rows(index, carry):
-            half, chunk = index // CHUNKS, index % CHUNKS
-            columns = pl.ds(pl.multiple_of(index * rows, LANES), rows)
-            turned[:, columns] = source[half, chunk_rows(chunk)].T
-            return carry
-
-        lax.fori_loop(0, 2 * CHUNKS, turn_rows, 0)
-
-    own_columns = pl.ds(pl.multiple_of(t * PIECE, LANES), PIECE)
-
-    for piece in range(WINDOW):
-        own_copy(piece).wait()
-        push(piece)
-    for chunk in range(CHUNKS):
-        place = x_low.at[0, t, chunk_rows(chunk)]
-        remote(
-            tokens_ref.at[chunk_rows(chunk)],
-            place,
-            x_send.at[0, chunk],
-            x_recv.at[0, chunk],
-            x_peer,
-        ).start()
     seg_q = seg_ref[...].astype(jnp.float32)
     half_lanes = pl.ds(pl.multiple_of(t * half_rows, LANES), half_rows)
     counted_rows = valid_ref[...] * (seg_ref[:, half_lanes] > 0).astype(jnp.int32)
@@ -461,11 +202,319 @@
     small_ref[pl.ds(14, layers), pl.ds(0, share)] = query_ref[...].astype(jnp.float32)
     small_ref[pl.ds(16, layers), pl.ds(0, ff_bias_ref.shape[1])] = ff_bias_ref[...].astype(jnp.float32)
     small_ref[pl.ds(18, 6)] = jnp.broadcast_to(count_local, (6, small_ref.shape[1]))
+    pl.semaphore_wait(barrier, len(everyone))
+
+    def remote(src, dst, send_sem, recv_sem, device):
+        return pltpu.make_async_remote_copy(
+            src_ref=src,
+            dst_ref=dst,
+            send_sem=send_sem,
+            recv_sem=recv_sem,
+            device_id=device,
+            device_id_type=MESH,
+        )
+
+    def z_copy(piece, step):
+        return remote(
+            mats.at[piece, z, y, c],
+            mats.at[piece, z, y, c],
+            z_send.at[piece, step],
+            z_recv.at[piece, step],
+            z_peers[step],
+        )
+
+    relays = (z == 1) | (z == 2)
+
+    def goes(step):
+        if step == 1:
+            return None
+        return (z != 0) if step == 2 else (z != 3)
+
+    def when(condition, action):
+        if condition is None:
+            action()
+        else:
+            pl.when(condition)(action)
+
+    def relay(piece):
+        source = jnp.where(z == 2, 0, 3)
+        block = mats.at[piece, source, y, c]
+        return remote(
+            block,
+            block,
+            z_send.at[piece, 3],
+            z_recv.at[piece, jnp.where(z == 2, 2, 0)],
+            peer(3 - source, y, c),
+        )
+
+    def push(piece):
+        for step in range(3):
+            when(goes(step), lambda step=step: z_copy(piece, step).start())
+
+    def relay_half(piece):
+        z_copy(piece, 1).wait_recv()
+        pl.when(relays)(lambda: relay(piece).start())
+
+    def hop_copy(piece, kind):
+        column = 1 - y if kind == 2 else y
+        block = mats.at[piece, :, column, c]
+        return remote(
+            block,
+            block,
+            hop_send.at[piece, kind],
+            hop_recv.at[piece, kind],
+            y_peer if kind == 0 else c_peer,
+        )
+
+    def small_z(step):
+        block = small_all.at[z, y, c]
+        return remote(small_ref, block, s_send.at[step], s_recv.at[step], z_peers[step])
+
+    def small_hop(kind):
+        column = 1 - y if kind == 2 else y
+        block = small_all.at[:, column, c]
+        return remote(
+            block, block, s_send.at[3 + kind], s_recv.at[3 + kind], y_peer if kind == 0 else c_peer
+        )
+
+    def first_half(piece):
+        z_copy(piece, 0).wait_recv()
+        z_copy(piece, 2).wait_recv()
+        if isinstance(piece, int):
+            if piece + WINDOW < pieces:
+                push(piece + WINDOW)
+        else:
+            pl.when(piece + WINDOW < pieces)(lambda: push(piece + WINDOW))
+        hop_copy(piece, 0).start()
+        hop_copy(piece, 1).start()
+
+    def second_half(piece):
+        hop_copy(piece, 0).wait_recv()
+        hop_copy(piece, 2).start()
+
+    def advance(step):
+        if isinstance(step, int):
+            if step == 0:
+                for piece in range(ROW_LEAD):
+                    relay_half(piece)
+                for piece in range(COL_LEAD):
+                    first_half(piece)
+            if step + ROW_LEAD < pieces:
+                relay_half(step + ROW_LEAD)
+            if step + COL_LEAD < pieces:
+                first_half(step + COL_LEAD)
+            if 0 < step <= pieces:
+                second_half(step - 1)
+        else:
+            pl.when(step + ROW_LEAD < pieces)(lambda: relay_half(step + ROW_LEAD))
+            pl.when(step + COL_LEAD < pieces)(lambda: first_half(step + COL_LEAD))
+            pl.when(step <= pieces)(lambda: second_half(step - 1))
+
+    def need(first, count=1):
+        for piece in range(first, first + count):
+            hop_copy(piece, 1).wait_recv()
+            hop_copy(piece, 2).wait_recv()
+
+    def chunk_rows(chunk):
+        if isinstance(chunk, int):
+            return pl.ds(chunk * rows, rows)
+        return pl.ds(pl.multiple_of(chunk * rows, rows), rows)
+
+    def put_wide(first, chunk, value):
+        for column in range(width // PIECE):
+            start = first + column * half_rows + chunk * rows
+            if not isinstance(start, int):
+                start = pl.multiple_of(start, 8)
+            out_ref[pl.ds(start, rows)] = value[:, column * PIECE : (column + 1) * PIECE]
+
+    def give_rows(number, chunk, block):
+        place = block.at[t, chunk_rows(chunk)]
+        return remote(place, place, x_send.at[number, chunk], x_recv.at[number, chunk], x_peer)
+
+    def give_part(number, chunk):
+        return remote(
+            out_part.at[chunk_rows(chunk)],
+            in_part.at[chunk_rows(chunk)],
+            x_send.at[number, chunk],
+            x_recv.at[number, chunk],
+            x_peer,
+        )
+
+    def put_part(number, previous, chunk, value):
+        if previous is not None:
+            give_part(previous, chunk).wait_send()
+        out_part[chunk_rows(chunk)] = value.astype(jnp.bfloat16)
+        give_part(number, chunk).start()
+
+    def place_part(index, number, previous, value):
+        chunk = index % CHUNKS
+
+        @pl.when(index < CHUNKS)
+        def _():
+            put_part(number, previous, chunk, value)
+
+        @pl.when(index >= CHUNKS)
+        def _():
+            own_part[chunk_rows(chunk)] = value
+
+    def core_copy(piece):
+        return remote(
+            mats.at[piece, :, :, 1 - c],
+            from_core.at[piece],
+            r_send.at[piece, 0],
+            r_recv.at[piece, 0],
+            c_peer,
+        )
+
+    def col_copy(piece):
+        return remote(
+            from_core.at[piece, :, 1 - y],
+            from_col.at[piece],
+            r_send.at[piece, 1],
+            r_recv.at[piece, 1],
+            y_peer,
+        )
+
+    def row_copy(piece, step):
+        return remote(
+            from_core.at[piece, (z + step + 1) % 4, y],
+            from_row.at[piece, step],
+            r_send.at[piece, 2 + step],
+            r_recv.at[piece, 2 + step],
+            z_peers[step],
+        )
+
+    def reduce_core(piece):
+        core_copy(piece).wait_recv()
+
+        def add_row(row, carry):
+            from_core[piece, row] = (
+                from_core[piece, row].astype(jnp.float32)
+                + mats[piece, row, :, c].astype(jnp.float32)
+            ).astype(jnp.bfloat16)
+            return carry
+
+        lax.fori_loop(0, 4, add_row, 0)
+        col_copy(piece).start()
+
+    def reduce_col(piece):
+        col_copy(piece).wait_recv()
+
+        def add_row(row, carry):
+            from_core[piece, row, y] = (
+                from_core[piece, row, y].astype(jnp.float32) + from_col[piece, row].astype(jnp.float32)
+            ).astype(jnp.bfloat16)
+            return carry
+
+        lax.fori_loop(0, 4, add_row, 0)
+        for step in range(3):
+            row_copy(piece, step).start()
+
+    def reduce_row(piece):
+        for step in range(3):
+            row_copy(piece, step).wait_recv()
+        total = from_core[piece, z, y].astype(jnp.float32)
+        for step in range(3):
+            total = total + from_row[piece, step].astype(jnp.float32)
+        out_ref[pl.ds(piece * total.shape[0], total.shape[0])] = total
+
+    def reduce_step(index):
+        if isinstance(index, int):
+            if index < pieces:
+                reduce_core(pieces - 1 - index)
+            if 0 <= index - LAG < pieces:
+                reduce_col(pieces - 1 - (index - LAG))
+            if 0 <= index - 2 * LAG < pieces:
+                reduce_row(pieces - 1 - (index - 2 * LAG))
+        else:
+            pl.when(index < pieces)(lambda: reduce_core(pieces - 1 - index))
+            pl.when((index >= LAG) & (index < pieces + LAG))(
+                lambda: reduce_col(pieces - 1 - (index - LAG))
+            )
+            pl.when(index >= 2 * LAG)(lambda: reduce_row(pieces - 1 - (index - 2 * LAG)))
+
+    def put_grad(piece, value):
+        mats[piece] = value.astype(jnp.bfloat16).reshape(mats.shape[1:])
+        core_copy(piece).start()
+
+    sum_blocks = ((8, 24), (0, 8))
+
+    def sum_copy(phase, step):
+        first, count = sum_blocks[phase]
+        part = sums_ref.at[pl.ds(first, count)]
+        slot = step if step < 3 else 3 + z
+        device = (c_peer, y_peer, x_peer)[step] if step < 3 else z_peers[step - 3]
+        return remote(
+            part,
+            sums_in.at[slot, pl.ds(first, count)],
+            a_send.at[phase, step],
+            a_recv.at[phase, step],
+            device,
+        )
+
+    def sum_start(phase, step):
+        if step < 3:
+            sum_copy(phase, step).start()
+            return
+        first, count = sum_blocks[phase]
+        for k in range(3, 6):
+            sum_copy(phase, k).start()
+        sums_in[3 + z, pl.ds(first, count)] = sums_ref[pl.ds(first, count)]
+
+    def sum_finish(phase, step):
+        first, count = sum_blocks[phase]
+        block = pl.ds(first, count)
+        if step < 3:
+            sum_copy(phase, step).wait()
+            sums_ref[block] = sums_ref[block] + sums_in[step, block]
+            return
+        for k in range(3, 6):
+            sum_copy(phase, k).wait()
+        sums_ref[block] = (sums_in[3, block] + sums_in[4, block]) + (
+            sums_in[5, block] + sums_in[6, block]
+        )
+
+    def add_sum(row, value, column=None):
+        if column is None:
+            sums_ref[pl.ds(row, 1)] += value
+        else:
+            sums_ref[pl.ds(row, 1), column] += value
+
+    def par(row):
+        return param[pl.ds(row, 1)]
+
+    def matrix(piece, count=1):
+        parts = [mats[piece + j].reshape(width, PIECE) for j in range(count)]
+        return parts[0] if count == 1 else jnp.concatenate(parts, axis=1)
+
+    def turn(source):
+        def turn_rows(index, carry):
+            half, chunk = index // CHUNKS, index % CHUNKS
+            columns = pl.ds(pl.multiple_of(index * rows, LANES), rows)
+            turned[:, columns] = source[half, chunk_rows(chunk)].T
+            return carry
+
+        lax.fori_loop(0, 2 * CHUNKS, turn_rows, 0)
+
+    own_columns = pl.ds(pl.multiple_of(t * PIECE, LANES), PIECE)
+
+    for step in range(3):
+        small_z(step).start()
+    for piece in range(WINDOW):
+        own_copy(piece).wait()
+        push(piece)
+    for chunk in range(CHUNKS):
+        place = x_low.at[0, t, chunk_rows(chunk)]
+        remote(
+            tokens_ref.at[chunk_rows(chunk)],
+            place,
+            x_send.at[0, chunk],
+            x_recv.at[0, chunk],
+            x_peer,
+        ).start()
     own_tokens.wait()
     stream[...] = x_low[0, t].astype(jnp.float32)
     small_all[z, y, c] = small_ref[...]
-    for step in range(3):
-        small_z(step).start()
     for piece in range(WINDOW, pieces):
         own_copy(piece).wait()
     seg_k = jnp.broadcast_to(seg_q, (8, length)).T[:, :1]
@@ -480,8 +529,10 @@
         small_z(step).wait_recv()
     small_hop(0).start()
     small_hop(1).start()
+    advance(0)
     small_hop(0).wait_recv()
     small_hop(2).start()
+    advance(1)
     small_hop(1).wait_recv()
     small_hop(2).wait_recv()
     param[...] = jnp.zeros_like(param)
@@ -551,9 +602,9 @@
                 pl.when(index == place)(lambda step=step: advance(step))
 
         if early:
-            advance(0)
             for j in range(3):
-                advance(j + 1)
+                if j > 0:
+                    advance(j + 1)
                 need(base + j)
                 project(t, j, 1)
         else:
@@ -648,7 +699,7 @@
         if layer == layers - 1:
             remote(count_mine, count_theirs, c_send.at[0], c_recv.at[0], x_peer).wait()
             count_all = (count_mine[...] + count_theirs[...])[2:3, :1]
-            count_ref[...] = jnp.broadcast_to(count_all, count_ref.shape)
+            out_ref[pl.ds(spots[3], 8)] = jnp.broadcast_to(count_all, (8, PIECE))
             loss_scale = token_total / count_all
         def end_rows(chunk, carry, layer=layer, ex=ex, pump=pump):
             where = chunk_rows(chunk)
@@ -665,7 +716,7 @@
                 x_low[layer + 1, t, where] = value.astype(jnp.bfloat16)
                 give_rows(ex + 4, chunk, x_low.at[layer + 1]).start()
             else:
-                mixed_ref[where] = value.astype(jnp.bfloat16)
+                put_wide(spots[1], chunk, value)
                 deviation = value - teacher_ref[where].astype(jnp.float32)
                 weighted = weight_ref[where] * deviation
                 add_sum(24, jnp.sum(weighted * deviation, axis=0, keepdims=True))
@@ -677,8 +728,9 @@
 
     def finish_gather(piece, carry):
         for k in range(3):
-            z_copy(piece, k).wait_send()
+            when(goes(k), lambda k=k: z_copy(piece, k).wait_send())
             hop_copy(piece, k).wait_send()
+        pl.when(relays)(lambda: relay(piece).wait_send())
         return carry
 
     lax.fori_loop(0, pieces, finish_gather, 0)
@@ -739,6 +791,7 @@
             return carry
 
         feed_back(t, everything)
+        own_part[...] = up_back(t, everything)
         lax.fori_loop(0, CHUNKS, feed_back_peer, 0)
 
         def mid_rows(chunk, layer=layer, ex=ex, sums_base=sums_base):
@@ -765,83 +818,92 @@
         def up_grad(j, layer=layer, base=base, pair_grad=pair_grad):
             pair_grad(base + 4 + j, turned[...], slope.at[layer], j)
 
+
+        def out_grad(layer=layer, base=base):
+            turn(d_low.at[layer, 1])
+            put_grad(base + 3, product(turned[...], heads[layer].reshape(length, PIECE)))
+
+        def in_grads(layer=layer, base=base):
+            turn(x_low.at[layer])
+            for j in range(2, -1, -1):
+                put_grad(base + j, product(turned[...], d_qkv[j].reshape(length, PIECE)))
+
+        def sum_move(step, last=last):
+            if not last:
+                if step > 0:
+                    sum_finish(0, step - 1)
+                sum_start(0, step)
+
+        def attend_back(half, first_step, opening, layer=layer):
+            def pair_back(pair, carry):
+                lanes = pair_lanes(pair)
+                keys_in, values_in = pair_rows(layer, 1, pair), pair_rows(layer, 2, pair)
+
+                def chunk_back(chunk, carry):
+                    where = chunk_rows(chunk)
+                    columns = pl.ds(pl.multiple_of(half * half_rows + chunk * rows, rows), rows)
+                    bias = mask[:, columns]
+                    bias = jnp.concatenate([bias, bias], axis=1)
+                    queries = split_heads(qkv[layer, 0, half, where, lanes])
+                    grads = split_heads(d_heads[half, where, lanes])
+                    scores = product_nt(keys_in, queries) + bias
+                    probs = jnp.exp(scores - log_sum[layer, pair, half, chunk])
+                    d_probs = product_nt(values_in, grads)
+                    delta = jnp.sum(probs * d_probs, axis=0, keepdims=True)
+                    d_scores = (probs * (d_probs - delta)).astype(jnp.bfloat16)
+                    double = pl.ds(pl.multiple_of(chunk * 2 * rows, LANES), 2 * rows)
+                    probs_all[:, double] = probs.astype(jnp.bfloat16)
+                    scores_all[:, double] = d_scores
+                    d_query = merge_heads(product(pair_turn[pair], d_scores)) * HEAD_DIM**-0.5
+                    d_qkv[0, half, where, lanes] = d_query.astype(jnp.bfloat16)
+                    return carry
+
+                lax.fori_loop(0, CHUNKS, chunk_back, 0)
+                query_list, grad_list = [], []
+                for chunk in range(CHUNKS):
+                    where = chunk_rows(chunk)
+                    query_list.append(split_heads(qkv[layer, 0, half, where, lanes]))
+                    grad_list.append(split_heads(d_heads[half, where, lanes]))
+                d_keys = product(scores_all[...], jnp.concatenate(query_list, axis=0))
+                d_values = product(probs_all[...], jnp.concatenate(grad_list, axis=0))
+                if opening:
+                    pair_sums[pair, 0] = d_keys
+                    pair_sums[pair, 1] = d_values
+                else:
+                    for which, total in ((1, d_keys), (2, d_values)):
+                        total = (total + pair_sums[pair, which - 1]).astype(jnp.bfloat16)
+                        d_qkv[which, :, :, lanes] = total.reshape(2, half_rows, LANES)
+                pl.when(pair != 1)(lambda: reduce_step(first_step + pair // 2))
+                return carry
+
+            lax.fori_loop(0, pairs, pair_back, 0)
+
+        sum_move(0)
         turn(d_low.at[layer, 0])
-
-        def down_grads(index, carry, layer=layer, base=base, pair_grad=pair_grad):
-            j = ups - 2 - 2 * index
+        pair_grad(base + 8 + ups - 2, turned[...], act.at[layer], ups - 2)
+        mid_rows(0)
+        sum_move(1)
+        for j in range(ups - 4, -1, -2):
             pair_grad(base + 8 + j, turned[...], act.at[layer], j)
-            return carry
-
-        lax.fori_loop(0, ups // 2, down_grads, 0)
-        if not last:
-            sum_start(0, 0)
-        own_part[...] = up_back(t, everything)
-        mid_rows(0)
         reduce_step(done)
-        if not last:
-            sum_finish(0, 0)
-            sum_start(0, 1)
+        mid_rows(1)
+        sum_move(2)
+        reduce_step(done + 1)
         turn(h_low.at[layer])
-        up_grad(ups - 2)
-        mid_rows(1)
-        reduce_step(done + 1)
-        if not last:
-            sum_finish(0, 1)
-            sum_start(0, 2)
-        for j in range(ups - 4, -1, -2):
+        for j in range(ups - 2, -1, -2):
             up_grad(j)
+        reduce_step(done + 2)
+        sum_move(3)
         d_heads[t] = product(d_low[layer, 1, t], matrix(base + 3)).astype(jnp.bfloat16)
         for pair in range(pairs):
             pair_turn[pair] = pair_rows(layer, 1, pair).T
-        reduce_step(done + 2)
-        if not last:
-            sum_finish(0, 2)
-            sum_start(0, 3)
-        reduce_step(done + 3)
+        attend_back(t, done + 3, True)
         for chunk in range(CHUNKS):
             give_rows(ex + 2, chunk, d_low.at[layer, 1]).wait_recv()
         d_heads[1 - t] = product(d_low[layer, 1, 1 - t], matrix(base + 3)).astype(jnp.bfloat16)
-
-        def pair_back(pair, carry, layer=layer, done=done):
-            lanes = pair_lanes(pair)
-            keys_in, values_in = pair_rows(layer, 1, pair), pair_rows(layer, 2, pair)
-
-            def attend_back(index, carry, layer=layer, pair=pair, lanes=lanes, done=done):
-                spent = pair * 2 * CHUNKS + index
-                pl.when(spent % 3 == 2)(lambda: reduce_step(done + 4 + spent // 3))
-                half, chunk = index // CHUNKS, index % CHUNKS
-                where = chunk_rows(chunk)
-                columns = pl.ds(pl.multiple_of(index * rows, rows), rows)
-                bias = mask[:, columns]
-                bias = jnp.concatenate([bias, bias], axis=1)
-                keys_in, values_in = pair_rows(layer, 1, pair), pair_rows(layer, 2, pair)
-                queries = split_heads(qkv[layer, 0, half, where, lanes])
-                grads = split_heads(d_heads[half, where, lanes])
-                scores = product_nt(keys_in, queries) + bias
-                probs = jnp.exp(scores - log_sum[layer, pair, half, chunk])
-                d_probs = product_nt(values_in, grads)
-                delta = jnp.sum(probs * d_probs, axis=0, keepdims=True)
-                d_scores = (probs * (d_probs - delta)).astype(jnp.bfloat16)
-                double = pl.ds(pl.multiple_of(index * 2 * rows, LANES), 2 * rows)
-                probs_all[:, double] = probs.astype(jnp.bfloat16)
-                scores_all[:, double] = d_scores
-                d_query = merge_heads(product(pair_turn[pair], d_scores)) * HEAD_DIM**-0.5
-                d_qkv[0, half, where, lanes] = d_query.astype(jnp.bfloat16)
-                return carry
-
-            lax.fori_loop(0, 2 * CHUNKS, attend_back, 0)
-            query_list, grad_list = [], []
-            for index in range(2 * CHUNKS):
-                half, where = index // CHUNKS, chunk_rows(index % CHUNKS)
-                query_list.append(split_heads(qkv[layer, 0, half, where, lanes]))
-                grad_list.append(split_heads(d_heads[half, where, lanes]))
-            d_keys = product(scores_all[...], jnp.concatenate(query_list, axis=0))
-            d_values = product(probs_all[...], jnp.concatenate(grad_list, axis=0))
-            d_qkv[1, :, :, lanes] = d_keys.astype(jnp.bfloat16).reshape(2, half_rows, LANES)
-            d_qkv[2, :, :, lanes] = d_values.astype(jnp.bfloat16).reshape(2, half_rows, LANES)
-            return carry
-
-        lax.fori_loop(0, pairs, pair_back, 0)
+        attend_back(1 - t, done + 5, False)
+        if not last:
+            out_grad()
 
         def query_parts(index, carry, layer=layer, base=base, ex=ex):
             half, chunk = half_of(index), index % CHUNKS
@@ -864,20 +926,18 @@
         if not last:
             sum_start(1, 0)
         lax.fori_loop(0, 2 * CHUNKS, query_parts, 0)
-        turn(d_low.at[layer, 1])
-        put_grad(base + 3, product(turned[...], heads[layer].reshape(length, PIECE)))
-        turn(x_low.at[layer])
-        for j in range(2, -1, -1):
-            put_grad(base + j, product(turned[...], d_qkv[j].reshape(length, PIECE)))
+        reduce_step(done + 7)
+        if last:
+            out_grad()
+        in_grads()
         reduce_step(done + 8)
-
     sum_finish(1, 0)
     sum_start(1, 1)
     ex = 8 * layers - 1
     for chunk in range(CHUNKS):
         where = chunk_rows(chunk)
         give_part(ex, chunk).wait_recv()
-        tokens_grad_ref[where] = stream[where] + own_part[where] + in_part[where].astype(jnp.float32)
+        put_wide(spots[0], chunk, stream[where] + own_part[where] + in_part[where].astype(jnp.float32))
     sum_finish(0, 3)
     sum_finish(1, 1)
     sum_start(1, 2)
@@ -891,6 +951,8 @@
 
     lax.fori_loop(pieces - 2, pieces + 2 * LAG, drain, 0)
     sum_finish(1, 3)
+    for column in range(width // PIECE):
+        out_ref[pl.ds(spots[2] + column * 32, 32)] = sums_ref[:, column * PIECE : (column + 1) * PIECE]
 
     for step in range(3):
         small_z(step).wait_send()
@@ -940,15 +1002,9 @@
         body = kernel
     return pl.pallas_call(
         body,
-        out_shape=(
-            jax.ShapeDtypeStruct((rows, width), low),
-            jax.ShapeDtypeStruct((rows, width), full),
-            jax.ShapeDtypeStruct((pieces, share, PIECE), full),
-            jax.ShapeDtypeStruct((32, width), full),
-            jax.ShapeDtypeStruct((8, LANES), full),
-        ),
+        out_shape=jax.ShapeDtypeStruct((places(pieces * share, rows)[4], PIECE), full),
         in_specs=[pl.BlockSpec(memory_space=pl.ANY)] * 5 + [vmem] * (len(operands) - 5),
-        out_specs=(vmem,) * 5,
+        out_specs=vmem,
         scratch_shapes=[
             pltpu.VMEM((pieces, *blocks), low),
             pltpu.VMEM((4, 2, 2, 24, 2 * LANES), full),
@@ -975,15 +1031,17 @@
             pltpu.VMEM((2, rows, PIECE), low),
             pltpu.VMEM((length, length), full),
             pltpu.VMEM((pairs, LANES, length), low),
-            pltpu.VMEM((length, 2 * length), low),
-            pltpu.VMEM((length, 2 * length), low),
+            pltpu.VMEM((length, length), low),
+            pltpu.VMEM((length, length), low),
+            pltpu.VMEM((pairs, 2, length, LANES), full),
             pltpu.VMEM((width, length), low),
             pltpu.VMEM((7, 32, width), full),
+            pltpu.VMEM((32, width), full),
             pltpu.VMEM((8, LANES), full),
             pltpu.VMEM((8, LANES), full),
             pltpu.VMEM((24, 2 * LANES), full),
             pltpu.VMEM((rows, 1), full),
-            dma((pieces, 3)),
+            dma((pieces, 4)),
             dma((pieces, 3)),
             dma((pieces, 3)),
             dma((pieces, 3)),
@@ -1027,11 +1085,7 @@
 
 def finish_kernel(
     place_count,
-    mixed_hbm,
-    tokens_grad_hbm,
-    grad_hbm,
-    sums_hbm,
-    count_hbm,
+    all_ref,
     mixed_out,
     tokens_grad_out,
     loss_out,
@@ -1044,38 +1098,32 @@
     ff_bias_out,
     query_out,
     sums_ref,
-    count_ref,
-    sem,
 ):
-    layers = attn_in_out.shape[0]
-    width = sums_ref.shape[1]
-    per_layer = grad_hbm.shape[0] // layers
-    ups = (per_layer - 4) // 2
-    moves = [
-        (sums_hbm, sums_ref),
-        (count_hbm, count_ref),
-        (mixed_hbm, mixed_out),
-        (tokens_grad_hbm, tokens_grad_out),
-    ]
+    layers, share = attn_out_out.shape[0], attn_out_out.shape[1]
+    rows, width = mixed_out.shape
+    ups = ff_in_out.shape[2] // PIECE
+    per_layer = 4 + 2 * ups
+    spots = places(layers * per_layer * share, rows)
+
+    def grad(piece):
+        return all_ref[pl.ds(piece * share, share)]
+
+    for column in range(width // PIECE):
+        lanes = pl.ds(column * PIECE, PIECE)
+        tokens_grad_out[:, lanes] = all_ref[pl.ds(spots[0] + column * rows, rows)]
+        mixed_out[:, lanes] = all_ref[pl.ds(spots[1] + column * rows, rows)].astype(mixed_out.dtype)
+        sums_ref[:, lanes] = all_ref[pl.ds(spots[2] + column * 32, 32)]
     for layer in range(layers):
         base = layer * per_layer
         for j in range(3):
-            moves.append((grad_hbm.at[base + j], attn_in_out.at[layer, j]))
-        moves.append((grad_hbm.at[base + 3], attn_out_out.at[layer]))
+            attn_in_out[layer, j] = grad(base + j)
+        attn_out_out[layer] = grad(base + 3)
         for j in range(ups):
             lanes = pl.ds(j * PIECE, PIECE)
-            moves.append((grad_hbm.at[base + 4 + j], ff_in_out.at[layer, :, lanes]))
-            moves.append((grad_hbm.at[base + 4 + ups + j], ff_out_out.at[layer, :, lanes]))
-    copies = [
-        pltpu.make_async_copy(source, target, sem.at[number])
-        for number, (source, target) in enumerate(moves)
-    ]
-    for copy in copies:
-        copy.start()
-    copies[0].wait()
-    copies[1].wait()
+            ff_in_out[layer, :, lanes] = grad(base + 4 + j)
+            ff_out_out[layer, :, lanes] = grad(base + 4 + ups + j)
     squares = jnp.sum(sums_ref[pl.ds(24, 1)], axis=1, keepdims=True)
-    loss_out[...] = squares / (count_ref[:1, :1] * width)
+    loss_out[...] = squares / (all_ref[pl.ds(spots[3], 8)][:1, :1] * width)
     place = lax.axis_index("fsdp")
     share = width // place_count
     own = pltpu.roll(sums_ref[:16], (width - place * share) % width, 1)[:, :share]
@@ -1088,8 +1136,6 @@
         query_out[pl.ds(layer, 1)] = own[layer * 8 + 7 : layer * 8 + 8]
         row = jnp.broadcast_to(sums_ref[pl.ds(16 + layer * 4 + first // width, 1)], (8, width))
         ff_bias_out[pl.ds(layer, 1)] = pltpu.roll(row, (width - first % width) % width, 1)[:1, :up_share]
-    for copy in copies[2:]:
-        copy.wait()
 
 
 def on_device(
@@ -1129,7 +1175,7 @@
         own_seg = lax.dynamic_slice_in_dim(segments, lax.axis_index("tp") * rows_dev, rows_dev, 1)
         total = sum_siblings(jnp.sum((valid * (own_seg > 0)).astype(jnp.float32)), extra)
         counted = jnp.broadcast_to(total, (8, LANES))
-    mixed, tokens_grad, grads, sums, count = run_step(
+    results = run_step(
         extra,
         float(length * size),
         matrices,
@@ -1141,15 +1187,24 @@
         counted,
     )
     if extra > 1:
+        share = width // GROUP
+        spots = places(results.shape[0] - places(0, rows_dev)[4], rows_dev)
         grads = lax.psum_scatter(
-            grads, "fsdp", scatter_dimension=1, axis_index_groups=sibling_groups(extra), tiled=True
-        )
-        sums = sum_siblings(sums, extra)
+            results[: spots[0]].reshape(-1, share, PIECE),
+            "fsdp",
+            scatter_dimension=1,
+            axis_index_groups=sibling_groups(extra),
+            tiled=True,
+        )
+        sums = sum_siblings(results[spots[2] : spots[3]], extra)
+        results = jnp.concatenate(
+            [grads.reshape(-1, PIECE), results[spots[0] : spots[2]], sums, results[spots[3] :]], axis=0
+        )
     vmem = pl.BlockSpec(memory_space=pltpu.VMEM)
     full = jnp.float32
     shapes = [
-        jax.ShapeDtypeStruct(mixed.shape, jnp.bfloat16),
-        jax.ShapeDtypeStruct(tokens_grad.shape, full),
+        jax.ShapeDtypeStruct((rows_dev, width), jnp.bfloat16),
+        jax.ShapeDtypeStruct((rows_dev, width), full),
         jax.ShapeDtypeStruct((1, 1), full),
     ]
     turned_in = (layers, 3, attn_in.shape[1], PIECE)
@@ -1161,16 +1216,12 @@
     mixed, tokens_grad, loss, in_grad, out_grad, up_grad, down_grad, bias_grad, *rest = pl.pallas_call(
         functools.partial(finish_kernel, size),
         out_shape=tuple(shapes),
-        in_specs=[pl.BlockSpec(memory_space=pltpu.HBM)] * 5,
+        in_specs=[vmem],
         out_specs=(vmem,) * len(shapes),
-        scratch_shapes=[
-            pltpu.VMEM(sums.shape, full),
-            pltpu.VMEM(count.shape, full),
-            pltpu.SemaphoreType.DMA((4 + grads.shape[0],)),
-        ],
+        scratch_shapes=[pltpu.VMEM((32, width), full)],
         compiler_params=pltpu.CompilerParams(vmem_limit_bytes=24 * 1024 * 1024),
         name="place_results",
-    )(mixed, tokens_grad, grads, sums, count)
+    )(results)
     return (
         mixed[None],
         tokens_grad[None],

time: 273 us -> 245 us (0.90)
  Pallas kernels: 266 us -> 239 us
  local copies, waits for them, and re-layouts: 5.16 us -> 1.97 us
    pallas_call x1, Pallas kernels: 263 us -> 238 us  [run_step(): pl.pallas_call(body, out_shape=jax.ShapeDtypeStruct((places(pieces * shar...]
    unnamed x10 -> x2, local copies, waits for them, and re-layouts: 5.16 us -> 1.97 us
where the time goes in v1:
time: 245 us; the launch traced here: 242 us
  Pallas kernels  239 us (98%)
    pallas_call x1, Pallas kernels, run_step(): pl.pallas_call(body, out_shape=jax.ShapeDtypeStruct((places(pieces * shar...  238 us

profile of v1, /device:TPU:0, one launch (start us, length us, event | category | flops | bytes accessed | tf_op | source)
XLA Modules:
  0.0 242.4 jit_solution(2995309508151944489)
XLA Ops:
  0.6 237.6 %encoder_step.1.all_ref = f32[2248,384]{1,0:T(8,128)} custom-call(bf16[2,3,48,384]{3,2,1,0:T(8,128)(2,1)} %bitcast.11, bf16[2,48,384]{2,1,0:T(8,128)(2,1)} %refs_1_.1, bf16[2,48,1536]{2,1,0:T(8,128)(2,1)} %refs_2_.1, bf16[2,48,1536]{2,1,0:T(8,128)(2,1)} %refs_3_.1, bf16[256,768]{1,0:T(8,128)(2,1)} %bitcast.9, bf16[5,2,48]{2,1,0:T(2,128)(2,1)} %bitcast.12, ...), custom_call_target="tpu_custom_call" | custom-call | tf_op jit(solution)/shard_map/encoder_step/pallas_call | solution.py:1003
  238.3 0.0 copy-start
  238.3 2.0 copy-done
  240.3 1.7 place_results.1
Async XLA Ops:
  238.3 2.0 copy-start

commit v2 on v1

--- a/solution.py
+++ b/solution.py
@@ -13,7 +13,7 @@
 CHUNKS = 2
 LANES = 128
 GROUP = 16
-WINDOW = 3
+WINDOW = 2
 ROW_LEAD = 2
 COL_LEAD = 1
 PUMPS = (
@@ -33,7 +33,8 @@
         "projected": (19,),
         "attend": ((2, 20),),
         "norm": ((0, 21), (1, 22)),
-        "feed": ((0, 23), (1, 24)),
+        "feed": ((0, 23),),
+        "fed": (24,),
     },
 )
 LAG = 2
@@ -88,6 +89,7 @@
     valid_ref,
     seg_ref,
     count_in_ref,
+    result_ref,
     out_ref,
     mats,
     small_all,
@@ -139,6 +141,7 @@
     a_recv,
     c_send,
     c_recv,
+    out_sem,
 ):
     pieces = mats.shape[0]
     spots = places(pieces * mats.shape[4], teacher_ref.shape[0])
@@ -254,6 +257,11 @@
     def relay_half(piece):
         z_copy(piece, 1).wait_recv()
         pl.when(relays)(lambda: relay(piece).start())
+        if isinstance(piece, int):
+            if piece + WINDOW < pieces:
+                push(piece + WINDOW)
+        else:
+            pl.when(piece + WINDOW < pieces)(lambda: push(piece + WINDOW))
 
     def hop_copy(piece, kind):
         column = 1 - y if kind == 2 else y
@@ -280,11 +288,6 @@
     def first_half(piece):
         z_copy(piece, 0).wait_recv()
         z_copy(piece, 2).wait_recv()
-        if isinstance(piece, int):
-            if piece + WINDOW < pieces:
-                push(piece + WINDOW)
-        else:
-            pl.when(piece + WINDOW < pieces)(lambda: push(piece + WINDOW))
         hop_copy(piece, 0).start()
         hop_copy(piece, 1).start()
 
@@ -672,14 +675,22 @@
                 act[layer, half, where, lanes] = (u * cdf).astype(jnp.bfloat16)
                 slope[layer, half, where, lanes] = (cdf + u * bell).astype(jnp.bfloat16)
 
-        def feed_peer(chunk, carry, layer=layer, ex=ex, feed=feed, pump=pump):
+        def down(half, where, layer=layer, base=base):
+            return product_nt(act[layer, half, where], matrix(base + 8, ups))
+
+        def feed_peer(chunk, carry, layer=layer, base=base, ex=ex, feed=feed, down=down, pump=pump):
             pump("feed", chunk)
             give_rows(ex + 2, chunk, h_low.at[layer]).wait_recv()
             feed(1 - t, chunk_rows(chunk))
+            if layer > 0:
+
+                @pl.when(chunk == 0)
+                def _():
+                    pump("fed")
+                    need(base + 8, 4)
+
+                put_part(ex + 3, ex + 1, chunk, down(1 - t, chunk_rows(chunk)))
             return carry
-
-        def down(half, where, layer=layer, base=base):
-            return product_nt(act[layer, half, where], matrix(base + 8, ups))
 
         def down_peer(chunk, carry, down=down, ex=ex):
             put_part(ex + 3, ex + 1, chunk, down(1 - t, chunk_rows(chunk)))
@@ -689,9 +700,10 @@
         pump("feed own")
         feed(t, everything)
         lax.fori_loop(0, CHUNKS, feed_peer, 0)
-        pump("fed")
-        need(base + 8, 4)
-        lax.fori_loop(0, CHUNKS, down_peer, 0)
+        if layer == 0:
+            pump("fed")
+            need(base + 8, 4)
+            lax.fori_loop(0, CHUNKS, down_peer, 0)
         pump("sent")
         own_part[...] = down(t, everything)
         pump("kept")
@@ -825,8 +837,13 @@
 
         def in_grads(layer=layer, base=base):
             turn(x_low.at[layer])
-            for j in range(2, -1, -1):
+
+            def one(index, carry):
+                j = 2 - index
                 put_grad(base + j, product(turned[...], d_qkv[j].reshape(length, PIECE)))
+                return carry
+
+            lax.fori_loop(0, 3, one, 0)
 
         def sum_move(step, last=last):
             if not last:
@@ -834,7 +851,16 @@
                     sum_finish(0, step - 1)
                 sum_start(0, step)
 
-        def attend_back(half, first_step, opening, layer=layer):
+        def attend_back(turn_number, carry, layer=layer, base=base, ex=ex, done=done):
+            half = jnp.where(turn_number == 0, t, 1 - t)
+
+            @pl.when(turn_number == 1)
+            def _():
+                for chunk in range(CHUNKS):
+                    give_rows(ex + 2, chunk, d_low.at[layer, 1]).wait_recv()
+
+            d_heads[half] = product(d_low[layer, 1, half], matrix(base + 3)).astype(jnp.bfloat16)
+
             def pair_back(pair, carry):
                 lanes = pair_lanes(pair)
                 keys_in, values_in = pair_rows(layer, 1, pair), pair_rows(layer, 2, pair)
@@ -866,17 +892,23 @@
                     grad_list.append(split_heads(d_heads[half, where, lanes]))
                 d_keys = product(scores_all[...], jnp.concatenate(query_list, axis=0))
                 d_values = product(probs_all[...], jnp.concatenate(grad_list, axis=0))
-                if opening:
+
+                @pl.when(turn_number == 0)
+                def _():
                     pair_sums[pair, 0] = d_keys
                     pair_sums[pair, 1] = d_values
-                else:
+
+                @pl.when(turn_number == 1)
+                def _():
                     for which, total in ((1, d_keys), (2, d_values)):
                         total = (total + pair_sums[pair, which - 1]).astype(jnp.bfloat16)
                         d_qkv[which, :, :, lanes] = total.reshape(2, half_rows, LANES)
-                pl.when(pair != 1)(lambda: reduce_step(first_step + pair // 2))
+
+                pl.when(pair != 1)(lambda: reduce_step(done + 3 + 2 * turn_number + pair // 2))
                 return carry
 
             lax.fori_loop(0, pairs, pair_back, 0)
+            return carry
 
         sum_move(0)
         turn(d_low.at[layer, 0])
@@ -890,27 +922,26 @@
         sum_move(2)
         reduce_step(done + 1)
         turn(h_low.at[layer])
-        for j in range(ups - 2, -1, -2):
-            up_grad(j)
+
+        def up_grads(index, carry, up_grad=up_grad):
+            up_grad(ups - 2 - 2 * index)
+            return carry
+
+        lax.fori_loop(0, ups // 2, up_grads, 0)
         reduce_step(done + 2)
         sum_move(3)
-        d_heads[t] = product(d_low[layer, 1, t], matrix(base + 3)).astype(jnp.bfloat16)
         for pair in range(pairs):
             pair_turn[pair] = pair_rows(layer, 1, pair).T
-        attend_back(t, done + 3, True)
-        for chunk in range(CHUNKS):
-            give_rows(ex + 2, chunk, d_low.at[layer, 1]).wait_recv()
-        d_heads[1 - t] = product(d_low[layer, 1, 1 - t], matrix(base + 3)).astype(jnp.bfloat16)
-        attend_back(1 - t, done + 5, False)
+        lax.fori_loop(0, 2, attend_back, 0)
         if not last:
             out_grad()
 
-        def query_parts(index, carry, layer=layer, base=base, ex=ex):
-            half, chunk = half_of(index), index % CHUNKS
-            where = chunk_rows(chunk)
+        def query_rows(half, where, base=base):
             parts = jnp.concatenate([d_qkv[j, half, where] for j in range(3)], axis=1)
-            part = product_nt(parts, matrix(base, 3))
-            place_part(index, ex + 3, ex + 1, part)
+            return product_nt(parts, matrix(base, 3))
+
+        def query_peer(chunk, carry, ex=ex, query_rows=query_rows):
+            put_part(ex + 3, ex + 1, chunk, query_rows(1 - t, chunk_rows(chunk)))
             return carry
 
         add_sum(
@@ -925,34 +956,45 @@
         )
         if not last:
             sum_start(1, 0)
-        lax.fori_loop(0, 2 * CHUNKS, query_parts, 0)
+        lax.fori_loop(0, CHUNKS, query_peer, 0)
+        own_part[...] = query_rows(t, everything)
         reduce_step(done + 7)
         if last:
             out_grad()
         in_grads()
         reduce_step(done + 8)
-    sum_finish(1, 0)
-    sum_start(1, 1)
+    def store(first, count, number):
+        block = pl.ds(first, count)
+        return pltpu.make_async_copy(out_ref.at[block], result_ref.at[block], out_sem.at[number])
+
+    later = per_layer * mats.shape[4]
+    stores = (
+        store(later, spots[0] - later, 0),
+        store(spots[0], spots[4] - spots[0], 1),
+        store(0, later, 2),
+    )
+    stores[0].start()
+    for step in range(3):
+        sum_finish(1, step)
+        sum_start(1, step + 1)
+        reduce_step(pieces - 3 + step)
     ex = 8 * layers - 1
     for chunk in range(CHUNKS):
         where = chunk_rows(chunk)
         give_part(ex, chunk).wait_recv()
         put_wide(spots[0], chunk, stream[where] + own_part[where] + in_part[where].astype(jnp.float32))
     sum_finish(0, 3)
-    sum_finish(1, 1)
-    sum_start(1, 2)
-    reduce_step(pieces - 3)
-    sum_finish(1, 2)
-    sum_start(1, 3)
+    sum_finish(1, 3)
+    for column in range(width // PIECE):
+        out_ref[pl.ds(spots[2] + column * 32, 32)] = sums_ref[:, column * PIECE : (column + 1) * PIECE]
+    stores[1].start()
 
     def drain(step, carry):
         reduce_step(step)
         return carry
 
-    lax.fori_loop(pieces - 2, pieces + 2 * LAG, drain, 0)
-    sum_finish(1, 3)
-    for column in range(width // PIECE):
-        out_ref[pl.ds(spots[2] + column * 32, 32)] = sums_ref[:, column * PIECE : (column + 1) * PIECE]
+    lax.fori_loop(pieces, pieces + 2 * LAG, drain, 0)
+    stores[2].start()
 
     for step in range(3):
         small_z(step).wait_send()
@@ -974,6 +1016,8 @@
         return carry
 
     lax.fori_loop(0, pieces, finish_grads, 0)
+    for copy in stores:
+        copy.wait()
 
 
 def run_step(extra, token_total, matrices, vectors, tokens, teacher, valid, seg_ids, counted):
@@ -1004,8 +1048,9 @@
         body,
         out_shape=jax.ShapeDtypeStruct((places(pieces * share, rows)[4], PIECE), full),
         in_specs=[pl.BlockSpec(memory_space=pl.ANY)] * 5 + [vmem] * (len(operands) - 5),
-        out_specs=vmem,
+        out_specs=pl.BlockSpec(memory_space=pl.ANY),
         scratch_shapes=[
+            pltpu.VMEM((places(pieces * share, rows)[4], PIECE), full),
             pltpu.VMEM((pieces, *blocks), low),
             pltpu.VMEM((4, 2, 2, 24, 2 * LANES), full),
             pltpu.VMEM((16, width), full),
@@ -1056,6 +1101,7 @@
             dma((2, 6)),
             dma((1,)),
             dma((1,)),
+            dma((3,)),
         ],
         compiler_params=pltpu.CompilerParams(
             collective_id=0, has_side_effects=True, vmem_limit_bytes=67_043_328

time: 245 us -> 237 us (0.967)
  Pallas kernels: 239 us -> 234 us
    pallas_call x1, Pallas kernels: 238 us -> 232 us  [run_step(): pl.pallas_call(body, out_shape=jax.ShapeDtypeStruct((places(pieces * shar...]
where the time goes in v2:
time: 237 us; the launch traced here: 236 us
  Pallas kernels  234 us (99%)
    pallas_call x1, Pallas kernels, run_step(): pl.pallas_call(body, out_shape=jax.ShapeDtypeStruct((places(pieces * shar...  232 us

profile of v2, /device:TPU:0, one launch (start us, length us, event | category | flops | bytes accessed | tf_op | source)
XLA Modules:
  0.0 236.5 jit_solution(12284704434612616031)
XLA Ops:
  0.6 232.2 %encoder_step.1.all_ref = f32[2248,384]{1,0:T(8,128)} custom-call(bf16[2,3,48,384]{3,2,1,0:T(8,128)(2,1)} %bitcast.11, bf16[2,48,384]{2,1,0:T(8,128)(2,1)} %refs_1_.1, bf16[2,48,1536]{2,1,0:T(8,128)(2,1)} %refs_2_.1, bf16[2,48,1536]{2,1,0:T(8,128)(2,1)} %refs_3_.1, bf16[256,768]{1,0:T(8,128)(2,1)} %bitcast.9, bf16[5,2,48]{2,1,0:T(2,128)(2,1)} %bitcast.12, ...), custom_call_target="tpu_custom_call" | custom-call | tf_op jit(solution)/shard_map/encoder_step/pallas_call | solution.py:1047
  232.8 0.0 copy-start
  232.8 2.0 copy-done
  234.8 1.7 place_results.1
Async XLA Ops:
  232.8 2.0 copy-start

commit v3 on v2

--- a/solution.py
+++ b/solution.py
@@ -38,6 +38,7 @@
     },
 )
 LAG = 2
+LATE = 6
 
 epsilon = 1e-05
 root_half = 0.7071067811865476
@@ -391,10 +392,7 @@
         core_copy(piece).wait_recv()
 
         def add_row(row, carry):
-            from_core[piece, row] = (
-                from_core[piece, row].astype(jnp.float32)
-                + mats[piece, row, :, c].astype(jnp.float32)
-            ).astype(jnp.bfloat16)
+            from_core[piece, row] = from_core[piece, row] + mats[piece, row, :, c]
             return carry
 
         lax.fori_loop(0, 4, add_row, 0)
@@ -404,9 +402,7 @@
         col_copy(piece).wait_recv()
 
         def add_row(row, carry):
-            from_core[piece, row, y] = (
-                from_core[piece, row, y].astype(jnp.float32) + from_col[piece, row].astype(jnp.float32)
-            ).astype(jnp.bfloat16)
+            from_core[piece, row, y] = from_core[piece, row, y] + from_col[piece, row]
             return carry
 
         lax.fori_loop(0, 4, add_row, 0)
@@ -427,14 +423,14 @@
                 reduce_core(pieces - 1 - index)
             if 0 <= index - LAG < pieces:
                 reduce_col(pieces - 1 - (index - LAG))
-            if 0 <= index - 2 * LAG < pieces:
-                reduce_row(pieces - 1 - (index - 2 * LAG))
+            if 0 <= index - LATE < pieces:
+                reduce_row(pieces - 1 - (index - LATE))
         else:
             pl.when(index < pieces)(lambda: reduce_core(pieces - 1 - index))
             pl.when((index >= LAG) & (index < pieces + LAG))(
                 lambda: reduce_col(pieces - 1 - (index - LAG))
             )
-            pl.when(index >= 2 * LAG)(lambda: reduce_row(pieces - 1 - (index - 2 * LAG)))
+            pl.when(index >= LATE)(lambda: reduce_row(pieces - 1 - (index - LATE)))
 
     def put_grad(piece, value):
         mats[piece] = value.astype(jnp.bfloat16).reshape(mats.shape[1:])
@@ -877,14 +873,15 @@
                     d_probs = product_nt(values_in, grads)
                     delta = jnp.sum(probs * d_probs, axis=0, keepdims=True)
                     d_scores = (probs * (d_probs - delta)).astype(jnp.bfloat16)
-                    double = pl.ds(pl.multiple_of(chunk * 2 * rows, LANES), 2 * rows)
+                    double = pl.ds(chunk * 2 * rows, 2 * rows)
                     probs_all[:, double] = probs.astype(jnp.bfloat16)
                     scores_all[:, double] = d_scores
                     d_query = merge_heads(product(pair_turn[pair], d_scores)) * HEAD_DIM**-0.5
                     d_qkv[0, half, where, lanes] = d_query.astype(jnp.bfloat16)
                     return carry
 
-                lax.fori_loop(0, CHUNKS, chunk_back, 0)
+                for chunk in range(CHUNKS):
+                    chunk_back(chunk, 0)
                 query_list, grad_list = [], []
                 for chunk in range(CHUNKS):
                     where = chunk_rows(chunk)
@@ -993,7 +990,7 @@
         reduce_step(step)
         return carry
 
-    lax.fori_loop(pieces, pieces + 2 * LAG, drain, 0)
+    lax.fori_loop(pieces, pieces + LATE, drain, 0)
     stores[2].start()
 
     for step in range(3):

time: 237 us -> 233 us (0.983)
  Pallas kernels: 234 us -> 230 us
    pallas_call x1, Pallas kernels: 232 us -> 228 us  [run_step(): pl.pallas_call(body, out_shape=jax.ShapeDtypeStruct((places(pieces * shar...]
where the time goes in v3:
time: 233 us; the launch traced here: 232 us
  Pallas kernels  230 us (99%)
    pallas_call x1, Pallas kernels, run_step(): pl.pallas_call(body, out_shape=jax.ShapeDtypeStruct((places(pieces * shar...  228 us

profile of v3, /device:TPU:0, one launch (start us, length us, event | category | flops | bytes accessed | tf_op | source)
XLA Modules:
  0.0 232.3 jit_solution(7525415450956058321)
XLA Ops:
  0.6 228.0 %encoder_step.1.all_ref = f32[2248,384]{1,0:T(8,128)} custom-call(bf16[2,3,48,384]{3,2,1,0:T(8,128)(2,1)} %bitcast.11, bf16[2,48,384]{2,1,0:T(8,128)(2,1)} %refs_1_.1, bf16[2,48,1536]{2,1,0:T(8,128)(2,1)} %refs_2_.1, bf16[2,48,1536]{2,1,0:T(8,128)(2,1)} %refs_3_.1, bf16[256,768]{1,0:T(8,128)(2,1)} %bitcast.9, bf16[5,2,48]{2,1,0:T(2,128)(2,1)} %bitcast.12, ...), custom_call_target="tpu_custom_call" | custom-call | tf_op jit(solution)/shard_map/encoder_step/pallas_call | solution.py:1044
  228.7 0.0 copy-start
  228.7 2.0 copy-done
  230.6 1.7 place_results.1
Async XLA Ops:
  228.7 2.0 copy-start

commit v4 on v3

--- a/solution.py
+++ b/solution.py
@@ -14,26 +14,25 @@
 LANES = 128
 GROUP = 16
 WINDOW = 2
-ROW_LEAD = 2
+ROW_LEAD = 1
 COL_LEAD = 1
 PUMPS = (
     {
         "projected": (4,),
-        "attend": ((1, 5), (2, 6)),
-        "norm": ((0, 7), (1, 8)),
-        "feed own": (9,),
-        "feed": ((0, 10),),
-        "fed": (11, 12),
+        "attend": ((2, 5), (3, 6)),
+        "norm": ((0, 7), (1, 8), (1, 9)),
+        "feed own": (10,),
+        "feed": ((0, 11),),
+        "fed": (12,),
         "sent": (13,),
-        "kept": (14,),
-        "end": ((0, 15), (1, 16)),
+        "kept": (14, 15),
+        "end": ((0, 16),),
     },
     {
         "own projected": (17, 18),
-        "projected": (19,),
-        "attend": ((2, 20),),
+        "attend": ((1, 19), (3, 20)),
         "norm": ((0, 21), (1, 22)),
-        "feed": ((0, 23),),
+        "feed own": (23,),
         "fed": (24,),
     },
 )

time: 233 us -> 233 us (level)
  no operation moved by 1% of the time
where the time goes in v4:
time: 233 us
  Pallas kernels  230 us (99%)
    pallas_call x1, Pallas kernels, run_step(): pl.pallas_call(body, out_shape=jax.ShapeDtypeStruct((places(pieces * shar...  229 us

profile of v4, /device:TPU:0, one launch (start us, length us, event | category | flops | bytes accessed | tf_op | source)
XLA Modules:
  0.0 233.0 jit_solution(4862780598760344359)
XLA Ops:
  0.6 228.6 %encoder_step.1.all_ref = f32[2248,384]{1,0:T(8,128)} custom-call(bf16[2,3,48,384]{3,2,1,0:T(8,128)(2,1)} %bitcast.11, bf16[2,48,384]{2,1,0:T(8,128)(2,1)} %refs_1_.1, bf16[2,48,1536]{2,1,0:T(8,128)(2,1)} %refs_2_.1, bf16[2,48,1536]{2,1,0:T(8,128)(2,1)} %refs_3_.1, bf16[256,768]{1,0:T(8,128)(2,1)} %bitcast.9, bf16[5,2,48]{2,1,0:T(2,128)(2,1)} %bitcast.12, ...), custom_call_target="tpu_custom_call" | custom-call | tf_op jit(solution)/shard_map/encoder_step/pallas_call | solution.py:1043
  229.3 0.0 copy-start
  229.3 2.0 copy-done
  231.3 1.7 place_results.1
Async XLA Ops:
  229.3 2.0 copy-start

commit v5 on v3

--- a/solution.py
+++ b/solution.py
@@ -14,7 +14,7 @@
 LANES = 128
 GROUP = 16
 WINDOW = 2
-ROW_LEAD = 2
+ROW_LEAD = 1
 COL_LEAD = 1
 PUMPS = (
     {

time: 233 us -> 232 us (level)
  no operation moved by 1% of the time
where the time goes in v5:
time: 232 us
  Pallas kernels  229 us (99%)
    pallas_call x1, Pallas kernels, run_step(): pl.pallas_call(body, out_shape=jax.ShapeDtypeStruct((places(pieces * shar...  227 us

profile of v5, /device:TPU:0, one launch (start us, length us, event | category | flops | bytes accessed | tf_op | source)
XLA Modules:
  0.0 231.6 jit_solution(16697619633625653044)
XLA Ops:
  0.6 227.3 %encoder_step.1.all_ref = f32[2248,384]{1,0:T(8,128)} custom-call(bf16[2,3,48,384]{3,2,1,0:T(8,128)(2,1)} %bitcast.11, bf16[2,48,384]{2,1,0:T(8,128)(2,1)} %refs_1_.1, bf16[2,48,1536]{2,1,0:T(8,128)(2,1)} %refs_2_.1, bf16[2,48,1536]{2,1,0:T(8,128)(2,1)} %refs_3_.1, bf16[256,768]{1,0:T(8,128)(2,1)} %bitcast.9, bf16[5,2,48]{2,1,0:T(2,128)(2,1)} %bitcast.12, ...), custom_call_target="tpu_custom_call" | custom-call | tf_op jit(solution)/shard_map/encoder_step/pallas_call | solution.py:1044
  227.9 0.0 copy-start
  227.9 2.0 copy-done
  229.9 1.7 place_results.1
Async XLA Ops:
  227.9 2.0 copy-start
